TPU v7x, 32 devices: a whole 2x2x4 slice. The times are simulated.
32 devices in a mesh: members: 2 (over x), band: 16 (over z, y, core).
Axes of the slice: x: 2, y: 2, z: 4, core: 2. Of those that a mesh axis runs over, the one named last changes fastest.
Arguments:
- grid_inputs: bfloat16 [96, 384, 256], P(('members', 'band')), parts along dimension 0, may hold values from -6 to 6
- stencil_prenorm_scale: float32 [256], replicated, may hold values from 0.1 to 1.9
- patch_kernel_profiles: float32 [48, 9, 27], P('band'), may hold values from -1.2 to 1.2
- channel_mixer_tensor: bfloat16 [2304, 256], replicated, may hold values from -0.125 to 0.125
- softmax_prenorm_scale: float32 [256], replicated, may hold values from 0.1 to 1.9
- probe_lookup_content_projector: bfloat16 [256, 768], replicated, may hold values from -0.375 to 0.375
- head_logit_scales: float32 [8], replicated, may hold values from 3 to 500
- final_projector: bfloat16 [256, 256], replicated, may hold values from -0.375 to 0.375
- azimuth_reaches: int32 [48, 5], P('band'), may hold values from 1 to 8, as said below
Outputs:
- encoded: bfloat16 [96, 384, 256], P(('members', 'band')), parts along dimension 0
There are 2 independent parts, one for each index of `members`. A program takes and returns all parts, laid end to end along the dimension named above; an argument that names none is the same for every part. Nothing has to cross between parts.
Inputs may be any that keep to these rules, and one draw needn't show every extreme that they name: azimuth_reaches[i, a] is the longitude reach of row i's disc in its row at offset a - 2; the rows at the poles reach 8.
All inputs are finite; a program needn't handle non-finite values.
Results may differ from a plain program's by a relative error of at most 0.025.
The roundings to bfloat16 on the way count: a program that leaves them out, or rounds other values in their place, can miss the bound.
Values may be sent and summed in bfloat16 or wider, within the bound.
No kernel may reach another device: no remote copies, remote signals or barrier semaphores. Data moves between devices by JAX's collectives and lax.ppermute only.
A program may use at most 64 MiB of HBM per device.

v0:
```python
import jax
import jax.numpy as jnp
from jax import lax
from jax.sharding import PartitionSpec as P

LONGITUDES = 384
HEAD_COUNT = 8
HEAD_WIDTH = 32
CHANNELS = 256
BASIS_COUNT = 9
CONV_REACH = 4
PATCH_LAT_EXTENT = 2
DISC_REACH = 8
QUERY_BLOCK = 48


EPSILON = 1e-06


def padded_2(block, sides, width):
    for axis, dim in sides:
        count = lax.axis_size(axis)
        forward = [(i, i + 1) for i in range(count - 1)]
        backward = [(target, source) for source, target in forward]
        low = lax.ppermute(
            lax.slice_in_dim(block, block.shape[dim] - width, None, axis=dim), axis, forward
        )
        high = lax.ppermute(lax.slice_in_dim(block, 0, width, axis=dim), axis, backward)
        block = jnp.concatenate([low, block, high], axis=dim)
    return block


def rms_norm(values, gain_vector):
    values = values.astype(jnp.float32)
    inverse = lax.rsqrt(jnp.mean(values * values, axis=-1, keepdims=True) + EPSILON)
    return values * inverse * gain_vector


def reflect(rim_rows):
    return jnp.roll(jnp.flip(rim_rows, axis=-3), rim_rows.shape[-2] // 2, axis=-2)


def fill_poles(padded, local_rows, rim_width):
    position = lax.axis_index("band")
    last_index = lax.axis_size("band") - 1
    upper = jnp.where(
        position == 0, reflect(local_rows[..., :rim_width, :, :]), padded[..., :rim_width, :, :]
    )
    lower = jnp.where(
        position == last_index,
        reflect(local_rows[..., -rim_width:, :, :]),
        padded[..., -rim_width:, :, :],
    )
    return jnp.concatenate([upper, padded[..., rim_width:-rim_width, :, :], lower], axis=-3)


def unit_heads(values):
    shaped = values.astype(jnp.float32).reshape(values.shape[:-1] + (HEAD_COUNT, HEAD_WIDTH))
    inverse = lax.rsqrt(jnp.sum(shaped * shaped, axis=-1, keepdims=True) + EPSILON)
    return (shaped * inverse).reshape(values.shape).astype(jnp.bfloat16)


def conv_filters(patch_kernel_profiles, azimuth_reaches):
    tap_count = 2 * CONV_REACH + 1
    offsets = jnp.abs(jnp.arange(tap_count, dtype=jnp.int32) - CONV_REACH)
    limits = azimuth_reaches[:, PATCH_LAT_EXTENT - 1 : PATCH_LAT_EXTENT + 2]
    visible = offsets[None, None, :] <= limits[:, :, None]
    shaped = patch_kernel_profiles.reshape(
        patch_kernel_profiles.shape[0], BASIS_COUNT, 3, tap_count
    )
    masked = jnp.where(visible[:, None], shaped, jnp.float32(0.0))
    return masked.astype(jnp.bfloat16).reshape(patch_kernel_profiles.shape)


def lon_taps(window):
    shifted = jnp.stack(
        [jnp.roll(window, CONV_REACH - offset, axis=1) for offset in range(2 * CONV_REACH + 1)],
        axis=1,
    )
    return shifted.reshape((-1,) + window.shape[1:])


def lon_windows(rim_rows):
    padded = jnp.concatenate(
        [rim_rows[:, -DISC_REACH:], rim_rows, rim_rows[:, : QUERY_BLOCK - DISC_REACH]], axis=1
    )
    blocks = padded.reshape(padded.shape[0], -1, QUERY_BLOCK, padded.shape[-1])
    windows = jnp.concatenate([blocks[:, :-1], blocks[:, 1:, : 2 * DISC_REACH]], axis=2)
    return windows.reshape(windows.shape[:3] + (HEAD_COUNT, HEAD_WIDTH))


def look_at_one_parallel(
    lone_probe_parallel,
    lookup_strip_parallels,
    content_strip_parallels,
    parallel_azimuth_reach,
    head_logit_scales,
):
    window_width = QUERY_BLOCK + 2 * DISC_REACH
    probe_tensor = lone_probe_parallel.reshape(-1, QUERY_BLOCK, HEAD_COUNT, HEAD_WIDTH)
    lookup_patch_neighbours = lon_windows(lookup_strip_parallels)
    value_windows = lon_windows(content_strip_parallels)
    similarity_logits = jnp.einsum(
        "kyge,wknge->kgywn",
        probe_tensor,
        lookup_patch_neighbours,
        preferred_element_type=jnp.float32,
    )
    similarity_logits = similarity_logits * head_logit_scales[None, :, None, None, None]
    positions = jnp.arange(QUERY_BLOCK, dtype=jnp.int32)
    columns = jnp.arange(window_width, dtype=jnp.int32)
    distance = jnp.abs(columns[None, :] - DISC_REACH - positions[:, None])
    visible = distance[:, None, :] <= parallel_azimuth_reach[None, :, None]
    similarity_logits = jnp.where(visible[None, None], similarity_logits, jnp.float32(-1e30))
    flattened = similarity_logits.reshape(similarity_logits.shape[:3] + (-1,))
    row_peak = jnp.max(flattened, axis=-1, keepdims=True)
    exponent = jnp.exp(flattened - row_peak)
    weights = (
        (exponent / jnp.sum(exponent, axis=-1, keepdims=True))
        .astype(jnp.bfloat16)
        .reshape(similarity_logits.shape)
    )
    mixture = jnp.einsum(
        "nhqaw,anwhd->nqhd", weights, value_windows, preferred_element_type=jnp.float32
    )
    return mixture.astype(jnp.bfloat16).reshape(LONGITUDES, CHANNELS)


def project(inputs, weight_part):
    product = jnp.dot(inputs.reshape(-1, CHANNELS), weight_part, preferred_element_type=jnp.float32)
    return product.astype(jnp.bfloat16).reshape(inputs.shape[:-1] + (weight_part.shape[1],))


def conv_rows(extended, filters, channel_mixer_tensor, count):

    def conv_row(present_parallel_number):
        window = lax.dynamic_slice_in_dim(extended, present_parallel_number, 3, 0)
        tap_stack = lon_taps(window)
        basis_sums = jnp.einsum(
            "kt,tjc->jkc",
            filters[present_parallel_number],
            tap_stack,
            preferred_element_type=jnp.float32,
        ).astype(jnp.bfloat16)
        return jnp.dot(
            basis_sums.reshape(LONGITUDES, -1),
            channel_mixer_tensor,
            preferred_element_type=jnp.float32,
        )

    return lax.map(conv_row, jnp.arange(count, dtype=jnp.int32))


def conv_section(
    grid_inputs,
    normed,
    received,
    filters,
    channel_mixer_tensor,
    softmax_prenorm_scale,
    probe_lookup_content_projector,
):
    extended = fill_poles(received, normed, 1)
    hidden = grid_inputs.astype(jnp.float32) + conv_rows(
        extended, filters, channel_mixer_tensor, grid_inputs.shape[0]
    )
    attn_in = rms_norm(hidden, softmax_prenorm_scale).astype(jnp.bfloat16)
    rescaled_probe = unit_heads(project(attn_in, probe_lookup_content_projector[:, :CHANNELS]))
    return (hidden, attn_in, rescaled_probe)


def on_device(
    grid_inputs,
    stencil_prenorm_scale,
    patch_kernel_profiles,
    channel_mixer_tensor,
    softmax_prenorm_scale,
    probe_lookup_content_projector,
    head_logit_scales,
    final_projector,
    azimuth_reaches,
):
    row_count = grid_inputs.shape[0]
    filters = conv_filters(patch_kernel_profiles, azimuth_reaches)
    normed = rms_norm(grid_inputs, stencil_prenorm_scale).astype(jnp.bfloat16)
    received = padded_2(normed, (("band", 0),), 1)
    hidden, attn_in, rescaled_probe = conv_section(
        grid_inputs,
        normed,
        received,
        filters,
        channel_mixer_tensor,
        softmax_prenorm_scale,
        probe_lookup_content_projector,
    )
    wide_rows = padded_2(attn_in, (("band", 0),), PATCH_LAT_EXTENT)
    wide_rows = fill_poles(wide_rows, attn_in, PATCH_LAT_EXTENT)
    kv_part = project(wide_rows, probe_lookup_content_projector[:, CHANNELS:])
    lookup_vectors_padded = unit_heads(kv_part[..., :CHANNELS])
    content_vectors_padded = kv_part[..., CHANNELS:]

    def attend_local(present_parallel_number):
        return look_at_one_parallel(
            lax.dynamic_index_in_dim(rescaled_probe, present_parallel_number, 0, keepdims=False),
            lax.dynamic_slice_in_dim(
                lookup_vectors_padded, present_parallel_number, 2 * PATCH_LAT_EXTENT + 1, 0
            ),
            lax.dynamic_slice_in_dim(
                content_vectors_padded, present_parallel_number, 2 * PATCH_LAT_EXTENT + 1, 0
            ),
            azimuth_reaches[present_parallel_number],
            head_logit_scales,
        )

    mixture = lax.map(attend_local, jnp.arange(row_count, dtype=jnp.int32))
    output = jnp.dot(
        mixture.reshape(-1, CHANNELS), final_projector, preferred_element_type=jnp.float32
    )
    return (hidden + output.reshape(hidden.shape)).astype(jnp.bfloat16)


def solution(mesh):
    placed = (
        P(("members", "band"), None, None),
        P(),
        P("band", None, None),
        P(),
        P(),
        P(),
        P(),
        P(),
        P("band", None),
    )
    return jax.shard_map(
        on_device,
        mesh=mesh,
        in_specs=placed,
        out_specs=P(("members", "band"), None, None),
        check_vma=False,
    )
```

profile of v0, /device:TPU:25, one launch (start us, length us, event | category | flops | bytes accessed | tf_op | source)
XLA Modules:
  0.0 208.5 jit_solution(6006632250594002056)
XLA Ops:
  2.7 3.7 %collective-permute-start = (bf16[1,384,256]{2,1,0:T(8,128)(2,1)S(1)}, bf16[1,384,256]{2,1,0:T(8,128)(2,1)S(1)}, u32[]{:S(2)}, u32[]{:S(2)}) collective-permute-start(bf16[1,384,256]{2,1,0:T(8,128)(2,1)S(1)} %get-tuple-element.236), channel_id=1, source_target_pairs={{0,1},{1,2},{2,3},{3,4},{4,5},{5,6},{6,7},{7,8},{8,9},{9,10},{10,1... | collective-permute-start | bytes 589832 | tf_op jit(solution)/shard_map/ppermute | solution.py:25
  6.4 1.9 collective-permute-start.1
  9.1 4.3 %collective-permute-done.1 = bf16[1,384,256]{2,1,0:T(8,128)(2,1)S(1)} collective-permute-done((bf16[1,384,256]{2,1,0:T(8,128)(2,1)S(1)}, bf16[1,384,256]{2,1,0:T(8,128)(2,1)S(1)}, u32[]{:S(2)}, u32[]{:S(2)}) %collective-permute-start.1) | collective-permute-done | bytes 196640 | tf_op jit(solution)/shard_map/ppermute | solution.py:28
  13.6 84.8 %while.22 = (s32[]{:T(128)}, f32[3,384,256]{2,1,0:T(8,128)}, s32[3]{0:T(128)S(1)}, bf16[5,384,256]{2,1,0:T(8,128)(2,1)S(1)}, bf16[3,9,27]{2,1,0:T(8,128)(2,1)S(1...) while((s32[]{:T(128)}, f32[3,384,256]{2,1,0:T(8,128)}, ...), condition=%wide.region_2.3_spmd, body=%wide.region_1.2_spmd.sunk | while | flops 511082496 | bytes 34019732 | solution.py:151
  20.3 2.1 fusion.74
  28.0 7.4 %convert_bitcast_fusion.2 = bf16[384,9,256]{2,1,0:T(8,128)(2,1)} fusion(bf16[27,384,256]{2,1,0:T(8,128)(2,1)} %bitcast.161, bf16[3,9,27]{2,1,0:T(8,128)(2,1)S(1)} %get-tuple-element.402, s32[]{:T(128)S(6)} %select_n.100), kind=kOutput, calls=%fused_computation.2.clone.1 | convolution fusion | flops 48660480 | bytes 7081988 | tf_op jit(solution)/shard_map/while/body/eval_jaxpr/kt,tjc->jkc/dot_general | solution.py:139
  35.4 3.8 %copy.144 = bf16[384,9,256]{0,2,1:T(8,128)(2,1)S(1)} copy(bf16[384,9,256]{2,1,0:T(8,128)(2,1)} %convert_bitcast_fusion.2) | data formatting | bytes 3538944 | tf_op jit(solution)/shard_map/while/body/eval_jaxpr/convert_element_type | solution.py:144
  39.2 2.7 %fusion.79 = f32[3,384,256]{2,1,0:T(8,128)} fusion(f32[3,384,256]{2,1,0:T(8,128)} %get-tuple-element.381, s32[]{:T(128)} %get-tuple-element.380, bf16[384,2304]{0,1:T(8,128)(2,1)S(1)} %bitcast.162, bf16[2304,256]{1,0:T(8,128)(2,1)} %get-tuple-element.403), kind=kOutput, calls=%fused_computation.4.clone.1 | convolution fusion | flops 452984832 | bytes 3342848 | tf_op jit(solution)/shard_map/while/body/eval_jaxpr/dot_general | solution.py:145
  48.6 2.1 fusion.74
  56.3 7.4 %convert_bitcast_fusion.2 = bf16[384,9,256]{2,1,0:T(8,128)(2,1)} fusion(bf16[27,384,256]{2,1,0:T(8,128)(2,1)} %bitcast.161, bf16[3,9,27]{2,1,0:T(8,128)(2,1)S(1)} %get-tuple-element.402, s32[]{:T(128)S(6)} %select_n.100), kind=kOutput, calls=%fused_computation.2.clone.1 | convolution fusion | flops 48660480 | bytes 7081988 | tf_op jit(solution)/shard_map/while/body/eval_jaxpr/kt,tjc->jkc/dot_general | solution.py:139
  63.6 3.8 %copy.144 = bf16[384,9,256]{0,2,1:T(8,128)(2,1)S(1)} copy(bf16[384,9,256]{2,1,0:T(8,128)(2,1)} %convert_bitcast_fusion.2) | data formatting | bytes 3538944 | tf_op jit(solution)/shard_map/while/body/eval_jaxpr/convert_element_type | solution.py:144
  67.5 2.7 %fusion.79 = f32[3,384,256]{2,1,0:T(8,128)} fusion(f32[3,384,256]{2,1,0:T(8,128)} %get-tuple-element.381, s32[]{:T(128)} %get-tuple-element.380, bf16[384,2304]{0,1:T(8,128)(2,1)S(1)} %bitcast.162, bf16[2304,256]{1,0:T(8,128)(2,1)} %get-tuple-element.403), kind=kOutput, calls=%fused_computation.4.clone.1 | convolution fusion | flops 452984832 | bytes 3342848 | tf_op jit(solution)/shard_map/while/body/eval_jaxpr/dot_general | solution.py:145
  76.8 2.1 fusion.74
  84.5 7.4 %convert_bitcast_fusion.2 = bf16[384,9,256]{2,1,0:T(8,128)(2,1)} fusion(bf16[27,384,256]{2,1,0:T(8,128)(2,1)} %bitcast.161, bf16[3,9,27]{2,1,0:T(8,128)(2,1)S(1)} %get-tuple-element.402, s32[]{:T(128)S(6)} %select_n.100), kind=kOutput, calls=%fused_computation.2.clone.1 | convolution fusion | flops 48660480 | bytes 7081988 | tf_op jit(solution)/shard_map/while/body/eval_jaxpr/kt,tjc->jkc/dot_general | solution.py:139
  91.9 3.8 %copy.144 = bf16[384,9,256]{0,2,1:T(8,128)(2,1)S(1)} copy(bf16[384,9,256]{2,1,0:T(8,128)(2,1)} %convert_bitcast_fusion.2) | data formatting | bytes 3538944 | tf_op jit(solution)/shard_map/while/body/eval_jaxpr/convert_element_type | solution.py:144
  95.7 2.7 %fusion.79 = f32[3,384,256]{2,1,0:T(8,128)} fusion(f32[3,384,256]{2,1,0:T(8,128)} %get-tuple-element.381, s32[]{:T(128)} %get-tuple-element.380, bf16[384,2304]{0,1:T(8,128)(2,1)S(1)} %bitcast.162, bf16[2304,256]{1,0:T(8,128)(2,1)} %get-tuple-element.403), kind=kOutput, calls=%fused_computation.4.clone.1 | convolution fusion | flops 452984832 | bytes 3342848 | tf_op jit(solution)/shard_map/while/body/eval_jaxpr/dot_general | solution.py:145
  103.1 1.9 collective-permute-start.2
  106.4 2.4 %collective-permute-start.3 = (bf16[2,384,256]{2,1,0:T(8,128)(2,1)}, bf16[2,384,256]{2,1,0:T(8,128)(2,1)}, u32[]{:S(2)}, u32[]{:S(2)}) collective-permute-start(bf16[2,384,256]{2,1,0:T(8,128)(2,1)} %get-tuple-element.231), channel_id=1, source_target_pairs={{1,0},{2,1},{3,2},{4,3},{5,4},{6,5},{7,6},{8,7},{9,8},{10,9},{11,1... | collective-permute-start | bytes 1179656 | tf_op jit(solution)/shard_map/ppermute | solution.py:28
  124.2 81.6 %while.23 = (s32[]{:T(128)}, bf16[3,384,256]{1,2,0:T(8,128)(2,1)}, s32[3]{0:T(128)S(1)}, bf16[7,384,256]{2,1,0:T(8,128)(2,1)}, s32[3,5]{1,0:T(4,128)S(1)}, /*ind...) while((s32[]{:T(128)}, bf16[3,384,256]{1,2,0:T(8,128)(2,1)}, ...), condition=%wide.region_9.10_spmd, body=%wide.region_6.9_spmd.sunk | while | flops 149519424 | bytes 76105208 | solution.py:215
  129.3 3.1 %copy.150 = bf16[5,8,64,256]{2,3,1,0:T(8,128)(2,1)S(1)} copy(bf16[5,8,64,256]{3,2,1,0:T(8,128)(2,1)} %pad_maximum_fusion.13) | data formatting | bytes 2621440 | tf_op jit(solution)/shard_map/while/body/eval_jaxpr/concatenate | solution.py:88
  137.3 2.2 %fusion.84 = f32[8,8,48]{2,1,0:T(8,128)S(1)} fusion(f32[8,8,48,5,64]{4,2,3,1,0:T(8,128)S(1)} %get-tuple-element.360, f32[8,8,48]{2,1,0:T(8,128)S(1)} %get-tuple-element.361, f32[8]{0:T(128)S(1)} %get-tuple-element.449, pred[48,5,64]{2,0,1:T(8,128)(4,1)S(1)} %broadcast_compare_fusion.3), kind=kLoop, calls=%fused_computation.44.clone.1 | loop fusion | flops 3929088 | bytes 3972128 | tf_op jit(solution)/shard_map/while/body/eval_jaxpr/reduce_sum | solution.py:119
  140.8 2.8 %copy.148 = bf16[5,8,64,256]{2,3,1,0:T(8,128)(2,1)} copy(bf16[5,8,64,256]{3,2,1,0:T(8,128)(2,1)S(1)} %pad_maximum_fusion.11) | data formatting | bytes 2621440 | tf_op jit(solution)/shard_map/while/body/eval_jaxpr/concatenate | solution.py:88
  143.6 6.4 %fusion.85 = bf16[8,8,32,48,1]{3,2,1,0,4:T(8,128)(2,1)S(1)} fusion(bf16[5,8,64,8,32]{2,4,3,1,0:T(8,128)(2,1)} %bitcast.167, f32[8,8,48,5,64]{4,2,3,1,0:T(8,128)} %copy-done.1, f32[8,8,48]{2,1,0:T(8,128)S(1)} %fusion.84, f32[8,8,48]{2,1,0:T(8,128)S(1)} %get-tuple-element.361, f32[8]{0:T(128)S(1)} %get-tuple-element.449, ...), kind=kOutput, calls=%fused_computation.45.clone.1 | convolution fusion | flops 67829760 | bytes 5479456 | tf_op jit(solution)/shard_map/while/body/eval_jaxpr/nhqaw,anwhd->nqhd/dot_general | solution.py:123
  156.5 3.1 %copy.150 = bf16[5,8,64,256]{2,3,1,0:T(8,128)(2,1)S(1)} copy(bf16[5,8,64,256]{3,2,1,0:T(8,128)(2,1)} %pad_maximum_fusion.13) | data formatting | bytes 2621440 | tf_op jit(solution)/shard_map/while/body/eval_jaxpr/concatenate | solution.py:88
  164.4 2.2 %fusion.84 = f32[8,8,48]{2,1,0:T(8,128)S(1)} fusion(f32[8,8,48,5,64]{4,2,3,1,0:T(8,128)S(1)} %get-tuple-element.360, f32[8,8,48]{2,1,0:T(8,128)S(1)} %get-tuple-element.361, f32[8]{0:T(128)S(1)} %get-tuple-element.449, pred[48,5,64]{2,0,1:T(8,128)(4,1)S(1)} %broadcast_compare_fusion.3), kind=kLoop, calls=%fused_computation.44.clone.1 | loop fusion | flops 3929088 | bytes 3972128 | tf_op jit(solution)/shard_map/while/body/eval_jaxpr/reduce_sum | solution.py:119
  168.0 2.8 %copy.148 = bf16[5,8,64,256]{2,3,1,0:T(8,128)(2,1)} copy(bf16[5,8,64,256]{3,2,1,0:T(8,128)(2,1)S(1)} %pad_maximum_fusion.11) | data formatting | bytes 2621440 | tf_op jit(solution)/shard_map/while/body/eval_jaxpr/concatenate | solution.py:88
  170.8 6.4 %fusion.85 = bf16[8,8,32,48,1]{3,2,1,0,4:T(8,128)(2,1)S(1)} fusion(bf16[5,8,64,8,32]{2,4,3,1,0:T(8,128)(2,1)} %bitcast.167, f32[8,8,48,5,64]{4,2,3,1,0:T(8,128)} %copy-done.1, f32[8,8,48]{2,1,0:T(8,128)S(1)} %fusion.84, f32[8,8,48]{2,1,0:T(8,128)S(1)} %get-tuple-element.361, f32[8]{0:T(128)S(1)} %get-tuple-element.449, ...), kind=kOutput, calls=%fused_computation.45.clone.1 | convolution fusion | flops 67829760 | bytes 5479456 | tf_op jit(solution)/shard_map/while/body/eval_jaxpr/nhqaw,anwhd->nqhd/dot_general | solution.py:123
  183.7 3.1 %copy.150 = bf16[5,8,64,256]{2,3,1,0:T(8,128)(2,1)S(1)} copy(bf16[5,8,64,256]{3,2,1,0:T(8,128)(2,1)} %pad_maximum_fusion.13) | data formatting | bytes 2621440 | tf_op jit(solution)/shard_map/while/body/eval_jaxpr/concatenate | solution.py:88
  191.6 2.2 %fusion.84 = f32[8,8,48]{2,1,0:T(8,128)S(1)} fusion(f32[8,8,48,5,64]{4,2,3,1,0:T(8,128)S(1)} %get-tuple-element.360, f32[8,8,48]{2,1,0:T(8,128)S(1)} %get-tuple-element.361, f32[8]{0:T(128)S(1)} %get-tuple-element.449, pred[48,5,64]{2,0,1:T(8,128)(4,1)S(1)} %broadcast_compare_fusion.3), kind=kLoop, calls=%fused_computation.44.clone.1 | loop fusion | flops 3929088 | bytes 3972128 | tf_op jit(solution)/shard_map/while/body/eval_jaxpr/reduce_sum | solution.py:119
  195.2 2.8 %copy.148 = bf16[5,8,64,256]{2,3,1,0:T(8,128)(2,1)} copy(bf16[5,8,64,256]{3,2,1,0:T(8,128)(2,1)S(1)} %pad_maximum_fusion.11) | data formatting | bytes 2621440 | tf_op jit(solution)/shard_map/while/body/eval_jaxpr/concatenate | solution.py:88
  198.0 6.4 %fusion.85 = bf16[8,8,32,48,1]{3,2,1,0,4:T(8,128)(2,1)S(1)} fusion(bf16[5,8,64,8,32]{2,4,3,1,0:T(8,128)(2,1)} %bitcast.167, f32[8,8,48,5,64]{4,2,3,1,0:T(8,128)} %copy-done.1, f32[8,8,48]{2,1,0:T(8,128)S(1)} %fusion.84, f32[8,8,48]{2,1,0:T(8,128)S(1)} %get-tuple-element.361, f32[8]{0:T(128)S(1)} %get-tuple-element.449, ...), kind=kOutput, calls=%fused_computation.45.clone.1 | convolution fusion | flops 67829760 | bytes 5479456 | tf_op jit(solution)/shard_map/while/body/eval_jaxpr/nhqaw,anwhd->nqhd/dot_general | solution.py:123
  205.7 2.8 %fusion.26 = bf16[3,384,256]{2,1,0:T(8,128)(2,1)} fusion(bf16[3,384,256]{1,2,0:T(8,128)(2,1)} %get-tuple-element.139, f32[3,384,256]{2,1,0:T(8,128)} %get-tuple-element.138, bf16[3,384,256]{2,1,0:T(8,128)(2,1)} %param.13, bf16[256,256]{1,0:T(8,128)(2,1)S(1)} %copy-done), kind=kOutput, calls=%fused_computation.79 | convolution fusion | flops 152174592 | bytes 3080192 | tf_op jit(solution)/shard_map/dot_general | solution.py:216
  (230 shorter events, 80.1 us)
Async XLA Ops:
  0.0 205.7 %copy-start = (bf16[256,256]{1,0:T(8,128)(2,1)S(1)}, bf16[256,256]{1,0:T(8,128)(2,1)}, u32[]{:S(2)}) copy-start(bf16[256,256]{1,0:T(8,128)(2,1)} %param.20) | copy-start | bytes 393220
  1.4 7.1 %copy-start.15 = (s32[3,5]{1,0:T(4,128)S(1)}, s32[3,5]{1,0:T(4,128)}, u32[]{:S(2)}) copy-start(s32[3,5]{1,0:T(4,128)} %param.21) | copy-start | bytes 184
  1.4 7.4 %copy-start.14 = (f32[3,9,27]{2,0,1:T(4,128)S(1)}, f32[3,9,27]{2,0,1:T(4,128)}, u32[]{:S(2)}) copy-start(f32[3,9,27]{2,0,1:T(4,128)} %param.15) | copy-start | bytes 8752
  2.7 6.3 %collective-permute-start = (bf16[1,384,256]{2,1,0:T(8,128)(2,1)S(1)}, bf16[1,384,256]{2,1,0:T(8,128)(2,1)S(1)}, u32[]{:S(2)}, u32[]{:S(2)}) collective-permute-start(bf16[1,384,256]{2,1,0:T(8,128)(2,1)S(1)} %get-tuple-element.236), channel_id=1, source_target_pairs={{0,1},{1,2},{2,3},{3,4},{4,5},{5,6},{6,7},{7,8},{8,9},{9,10},{10,1... | collective-permute-start | bytes 589832 | tf_op jit(solution)/shard_map/ppermute | solution.py:25
  6.4 7.0 %collective-permute-start.1 = (bf16[1,384,256]{2,1,0:T(8,128)(2,1)S(1)}, bf16[1,384,256]{2,1,0:T(8,128)(2,1)S(1)}, u32[]{:S(2)}, u32[]{:S(2)}) collective-permute-start(bf16[1,384,256]{2,1,0:T(8,128)(2,1)S(1)} %get-tuple-element.237), channel_id=1, source_target_pairs={{1,0},{2,1},{3,2},{4,3},{5,4},{6,5},{7,6},{8,7},{9,8},{10,9},{11,1... | collective-permute-start | bytes 589832 | tf_op jit(solution)/shard_map/ppermute | solution.py:28
  98.4 1.8 copy-start.5
  98.4 2.0 copy-start.6
  98.4 2.0 copy-start.16
  103.1 13.5 %collective-permute-start.2 = (bf16[2,384,256]{2,1,0:T(8,128)(2,1)}, bf16[2,384,256]{2,1,0:T(8,128)(2,1)}, u32[]{:S(2)}, u32[]{:S(2)}) collective-permute-start(bf16[2,384,256]{2,1,0:T(8,128)(2,1)} %get-tuple-element.230), channel_id=1, source_target_pairs={{0,1},{1,2},{2,3},{3,4},{4,5},{5,6},{6,7},{7,8},{8,9},{9,10},{10,1... | collective-permute-start | bytes 1179656 | tf_op jit(solution)/shard_map/ppermute | solution.py:25
  106.4 11.3 %collective-permute-start.3 = (bf16[2,384,256]{2,1,0:T(8,128)(2,1)}, bf16[2,384,256]{2,1,0:T(8,128)(2,1)}, u32[]{:S(2)}, u32[]{:S(2)}) collective-permute-start(bf16[2,384,256]{2,1,0:T(8,128)(2,1)} %get-tuple-element.231), channel_id=1, source_target_pairs={{1,0},{2,1},{3,2},{4,3},{5,4},{6,5},{7,6},{8,7},{9,8},{10,9},{11,1... | collective-permute-start | bytes 1179656 | tf_op jit(solution)/shard_map/ppermute | solution.py:28
  114.4 1.3 copy-start.7
  114.6 2.0 copy-start.9
  114.6 2.0 copy-start.10
  115.7 2.0 copy-start.8
  115.7 2.0 copy-start.11
  118.8 1.0 copy-start.12
  123.5 0.7 copy-start.13
  124.2 3.6 %copy-start.3 = (bf16[7,384,256]{1,2,0:T(8,128)(2,1)}, bf16[7,384,256]{1,2,0:T(8,128)(2,1)S(1)}, u32[]{:S(2)}) copy-start(bf16[7,384,256]{1,2,0:T(8,128)(2,1)S(1)} %get-tuple-element.448) | copy-start | bytes 4128772 | tf_op jit(solution)/shard_map/while
  137.2 3.1 %copy-start.1 = (f32[8,8,48,5,64]{4,2,3,1,0:T(8,128)}, f32[8,8,48,5,64]{4,2,3,1,0:T(8,128)S(1)}, u32[]{:S(2)}) copy-start(f32[8,8,48,5,64]{4,2,3,1,0:T(8,128)S(1)} %get-tuple-element.360) | copy-start | bytes 11796484 | tf_op jit(solution)/shard_map/while
  137.2 3.1 %copy-start.2 = (bf16[7,384,256]{2,1,0:T(8,128)(2,1)S(1)}, bf16[7,384,256]{2,1,0:T(8,128)(2,1)}, u32[]{:S(2)}) copy-start(bf16[7,384,256]{2,1,0:T(8,128)(2,1)} %get-tuple-element.445) | copy-start | bytes 4128772 | tf_op jit(solution)/shard_map/while
  150.0 1.4 copy-start.4
  151.4 3.6 %copy-start.3 = (bf16[7,384,256]{1,2,0:T(8,128)(2,1)}, bf16[7,384,256]{1,2,0:T(8,128)(2,1)S(1)}, u32[]{:S(2)}) copy-start(bf16[7,384,256]{1,2,0:T(8,128)(2,1)S(1)} %get-tuple-element.448) | copy-start | bytes 4128772 | tf_op jit(solution)/shard_map/while
  164.4 3.1 %copy-start.1 = (f32[8,8,48,5,64]{4,2,3,1,0:T(8,128)}, f32[8,8,48,5,64]{4,2,3,1,0:T(8,128)S(1)}, u32[]{:S(2)}) copy-start(f32[8,8,48,5,64]{4,2,3,1,0:T(8,128)S(1)} %get-tuple-element.360) | copy-start | bytes 11796484 | tf_op jit(solution)/shard_map/while
  164.4 3.1 %copy-start.2 = (bf16[7,384,256]{2,1,0:T(8,128)(2,1)S(1)}, bf16[7,384,256]{2,1,0:T(8,128)(2,1)}, u32[]{:S(2)}) copy-start(bf16[7,384,256]{2,1,0:T(8,128)(2,1)} %get-tuple-element.445) | copy-start | bytes 4128772 | tf_op jit(solution)/shard_map/while
  177.2 1.4 copy-start.4
  178.6 3.6 %copy-start.3 = (bf16[7,384,256]{1,2,0:T(8,128)(2,1)}, bf16[7,384,256]{1,2,0:T(8,128)(2,1)S(1)}, u32[]{:S(2)}) copy-start(bf16[7,384,256]{1,2,0:T(8,128)(2,1)S(1)} %get-tuple-element.448) | copy-start | bytes 4128772 | tf_op jit(solution)/shard_map/while
  191.6 3.1 %copy-start.1 = (f32[8,8,48,5,64]{4,2,3,1,0:T(8,128)}, f32[8,8,48,5,64]{4,2,3,1,0:T(8,128)S(1)}, u32[]{:S(2)}) copy-start(f32[8,8,48,5,64]{4,2,3,1,0:T(8,128)S(1)} %get-tuple-element.360) | copy-start | bytes 11796484 | tf_op jit(solution)/shard_map/while
  191.6 3.1 %copy-start.2 = (bf16[7,384,256]{2,1,0:T(8,128)(2,1)S(1)}, bf16[7,384,256]{2,1,0:T(8,128)(2,1)}, u32[]{:S(2)}) copy-start(bf16[7,384,256]{2,1,0:T(8,128)(2,1)} %get-tuple-element.445) | copy-start | bytes 4128772 | tf_op jit(solution)/shard_map/while
  204.4 1.4 copy-start.4
where the time goes:
time: 212 us; the launch traced here: 209 us
  local copies, waits for them, and re-layouts  67.7 us (32%)
  matrix products  59.8 us (28%)
  other arithmetic  46.4 us (22%)
  loops' own time  19.8 us (9%)
  starting transfers between devices  9.93 us (5%)
  waiting for transfers between devices  4.58 us (2%)
    while x21, other arithmetic  23 us
    dot_general x3, matrix products, conv_row(): jnp.einsum('kt,tjc->jkc', filters[present_parallel_number], tap_stack, pr...  22.1 us
    dot_general x3, matrix products, look_at_one_parallel(): jnp.einsum('nhqaw,anwhd->nqhd', weights, value_windows, preferred_element...  19.2 us
    concatenate x6, local copies, waits for them, and re-layouts, lon_windows(): jnp.concatenate([blocks[:, :-1], blocks[:, 1:, :2 * DISC_REACH]], axis=2)  17.7 us
    convert_element_type x3, local copies, waits for them, and re-layouts, conv_row(): basis_sums = jnp.einsum('kt,tjc->jkc', filters[present_parallel_number],...  11.5 us
    another operation x1, loops' own time, on_device(): mixture = lax.map(attend_local, jnp.arange(row_count, dtype=jnp.int32))  11 us
    another operation x1, loops' own time, conv_rows(): return lax.map(conv_row, jnp.arange(count, dtype=jnp.int32))  8.72 us
    dot_general x3, matrix products, conv_row(): jnp.dot(basis_sums.reshape(LONGITUDES, -1), channel_mixer_tensor, preferr...  8.11 us
  transfers between devices with their start and end apart: 4, of which 2 were waited for; matrix products, arithmetic and copies ran while one was open for 5% of the time, Pallas kernels for 0%

commit v1 on v0

v1 whole, which is shorter than its diff:
```python
import functools

import jax
import jax.numpy as jnp
from jax import lax
from jax.experimental import pallas as pl
from jax.experimental.pallas import tpu as pltpu
from jax.sharding import PartitionSpec as P

HEAD_COUNT = 8
HEAD_WIDTH = 32
BASIS_COUNT = 9
CONV_REACH = 4
PATCH_LAT_EXTENT = 2
DISC_REACH = 8
TAPS = 2 * CONV_REACH + 1
DISC_ROWS = 2 * PATCH_LAT_EXTENT + 1
EPSILON = 1e-06
HALO = PATCH_LAT_EXTENT + 1
BAND = 64
WINDOW = BAND + 16
QUERIES = 16
KEYS = QUERIES + 2 * DISC_REACH
FILTER_ROWS = 16
F32 = jnp.float32
BF16 = jnp.bfloat16


def scaled_norm(values, gain):
    inverse = lax.rsqrt(jnp.mean(values * values, axis=-1, keepdims=True) + EPSILON)
    return values * inverse * gain


def head_unit(values, ones):
    squares = values * values
    high = squares.astype(BF16)
    low = (squares - high.astype(F32)).astype(BF16)
    total = jnp.dot(high, ones, preferred_element_type=F32) + jnp.dot(
        low, ones, preferred_element_type=F32
    )
    return values * lax.rsqrt(total + EPSILON)


def wrapped(values, before, after):
    parts = [values[values.shape[0] - before :], values, values[:after]]
    return jnp.concatenate(parts, axis=0)


def window_kernel(
    rows,
    longitudes,
    flags,
    reaches,
    scales,
    local,
    low,
    high,
    flipped,
    conv_gain,
    mixer,
    attn_gain,
    projector,
    final,
    out,
    raw,
    normed,
    filters,
    bands,
    basis,
    hidden,
    attn_in,
    keys,
    values,
    queries,
    bias,
    mixture,
):
    channels = local.shape[1]
    half = longitudes // 2
    first = flags[0] > 0
    last = flags[1] > 0
    halo_base = HALO * longitudes

    def local_row(row):
        return local[row * longitudes : (row + 1) * longitudes, :]

    def rolled(row):
        block = local_row(row)
        return jnp.concatenate([block[half:], block[:half]], axis=0)

    for step in range(HALO):
        there = low[step * longitudes : (step + 1) * longitudes, :]
        raw[step] = jnp.where(first, rolled(HALO - 1 - step), there)
        there = high[step * longitudes : (step + 1) * longitudes, :]
        raw[HALO + rows + step] = jnp.where(last, rolled(rows - 1 - step), there)
    for row in range(rows):
        raw[HALO + row] = local_row(row)

    def norm_row(row, carry):
        block = scaled_norm(raw[row].astype(F32), conv_gain[...])
        normed[row] = wrapped(block, 8, 24).astype(BF16)
        return carry

    lax.fori_loop(0, rows + 2 * HALO, norm_row, 0)

    def filter_rows(ref, base, row):
        start = base + row * FILTER_ROWS
        return ref[start : start + FILTER_ROWS, :].astype(F32)

    for step in range(2):
        mine = filter_rows(flipped, 0, 1 - step)
        there = filter_rows(low, halo_base, 1 + step)
        filters[step] = jnp.where(first, mine, there)
        mine = filter_rows(flipped, 0, rows - 1 - step)
        there = filter_rows(high, halo_base, step)
        filters[2 + rows + step] = jnp.where(last, mine, there)
    for row in range(rows):
        filters[2 + row] = filter_rows(local, rows * longitudes, row)

    def conv_row(row, carry):
        for k in range(BASIS_COUNT):
            line = jnp.broadcast_to(filters[row, k : k + 1, :], (BAND, channels))
            line = pltpu.roll(line, 0, 1, stride=1, stride_axis=0)
            bands[k * BAND : (k + 1) * BAND, :] = line.astype(BF16)
        for block in range(longitudes // BAND):
            start = block * BAND
            window = jnp.concatenate(
                [
                    normed[row, start : start + WINDOW, :],
                    normed[row + 1, start : start + WINDOW, :],
                    normed[row + 2, start : start + WINDOW + 16, :],
                ],
                axis=0,
            )
            sums = jnp.dot(bands[...], window, preferred_element_type=F32).astype(BF16)
            for k in range(BASIS_COUNT):
                basis[start : start + BAND, k * channels : (k + 1) * channels] = sums[
                    k * BAND : (k + 1) * BAND
                ]
        total = raw[row + 1].astype(F32) + jnp.dot(
            basis[...], mixer[...], preferred_element_type=F32
        )
        hidden[row] = total
        attn_in[row] = scaled_norm(total, attn_gain[...]).astype(BF16)
        return carry

    lax.fori_loop(0, rows + 2 * PATCH_LAT_EXTENT, conv_row, 0)

    head_of_lane = lax.broadcasted_iota(jnp.int32, (channels, channels), 1) // HEAD_WIDTH
    head_of_row = lax.broadcasted_iota(jnp.int32, (channels, channels), 0) // HEAD_WIDTH
    ones = jnp.where(head_of_lane == head_of_row, 1.0, 0.0).astype(BF16)

    def key_row(row, carry):
        both = jnp.dot(
            attn_in[row], projector[:, channels : 3 * channels], preferred_element_type=F32
        )
        rounded = both.astype(BF16).astype(F32)
        unit = head_unit(rounded[:, :channels], ones)
        keys[row] = wrapped(unit, DISC_REACH, DISC_REACH).astype(BF16)
        values[row] = wrapped(rounded[:, channels:], DISC_REACH, DISC_REACH).astype(BF16)
        return carry

    lax.fori_loop(0, rows + 2 * PATCH_LAT_EXTENT, key_row, 0)

    lanes = HEAD_COUNT * QUERIES
    disc = DISC_ROWS * KEYS

    def query_row(row, carry):
        probe = jnp.dot(
            attn_in[row + PATCH_LAT_EXTENT],
            projector[:, :channels],
            preferred_element_type=F32,
        )
        queries[row] = head_unit(probe.astype(BF16).astype(F32), ones).astype(BF16)
        key_at = lax.broadcasted_iota(jnp.int32, (KEYS, lanes), 0)
        query_at = lax.broadcasted_iota(jnp.int32, (KEYS, lanes), 1) % QUERIES
        distance = jnp.abs(key_at - DISC_REACH - query_at)
        for a in range(DISC_ROWS):
            bias[row, a * KEYS : (a + 1) * KEYS, :] = jnp.where(
                distance <= reaches[row, a], 0.0, -1e30
            ).astype(F32)
        return carry

    lax.fori_loop(0, rows, query_row, 0)

    lane_head = lax.broadcasted_iota(jnp.int32, (1, lanes), 1) // QUERIES
    scale = jnp.zeros((1, lanes), F32)
    for h in range(HEAD_COUNT):
        scale = jnp.where(lane_head == h, scales[h], scale)
    channel_head = lax.broadcasted_iota(jnp.int32, (QUERIES, channels), 1) // HEAD_WIDTH

    unroll = 4
    per_row = longitudes // (QUERIES * unroll)

    def attend(step, carry):
        row = step // per_row
        base = (step % per_row) * (QUERIES * unroll)
        for u in range(unroll):
            start = pl.multiple_of(base + u * QUERIES, QUERIES)
            probe = queries[row, pl.ds(start, QUERIES), :]
            spread = jnp.concatenate(
                [jnp.where(channel_head == h, probe, jnp.zeros_like(probe)) for h in range(HEAD_COUNT)],
                axis=0,
            )
            near_keys = jnp.concatenate(
                [keys[row + a, pl.ds(start, KEYS), :] for a in range(DISC_ROWS)], axis=0
            )
            near_values = jnp.concatenate(
                [values[row + a, pl.ds(start, KEYS), :] for a in range(DISC_ROWS)], axis=0
            )
            scores = lax.dot_general(
                near_keys, spread, (((1,), (1,)), ((), ())), preferred_element_type=F32
            )
            scores = scores + bias[row]
            peak = jnp.max(scores, axis=0, keepdims=True)
            weights = jnp.exp((scores - peak) * scale)
            total = jnp.sum(weights, axis=0, keepdims=True)
            weights = (weights * (1.0 / total)).astype(BF16)
            mixed = lax.dot_general(
                weights, near_values, (((0,), (0,)), ((), ())), preferred_element_type=F32
            )
            result = jnp.zeros((QUERIES, channels), F32)
            for h in range(HEAD_COUNT):
                result = jnp.where(
                    channel_head == h, mixed[h * QUERIES : (h + 1) * QUERIES], result
                )
            mixture[row, pl.ds(start, QUERIES), :] = result.astype(BF16)
        return carry

    lax.fori_loop(0, rows * per_row, attend, 0)

    def finish(row, carry):
        product = jnp.dot(mixture[row], final[...], preferred_element_type=F32)
        out[row] = (hidden[row + PATCH_LAT_EXTENT] + product).astype(BF16)
        return carry

    lax.fori_loop(0, rows, finish, 0)


def filter_lines(profiles, reaches, flip):
    count = profiles.shape[0]
    offsets = jnp.abs(jnp.arange(TAPS, dtype=jnp.int32) - CONV_REACH)
    limits = reaches[:, PATCH_LAT_EXTENT - 1 : PATCH_LAT_EXTENT + 2]
    visible = offsets[None, None, :] <= limits[:, :, None]
    shaped = profiles.reshape(count, BASIS_COUNT, 3, TAPS)
    masked = jnp.where(visible[:, None], shaped, 0.0).astype(BF16)
    if flip:
        masked = masked[:, :, ::-1, :]
    edge = WINDOW - BAND - TAPS - CONV_REACH
    lines = jnp.pad(masked, ((0, 0), (0, 0), (0, 0), (CONV_REACH, BAND + edge)))
    lines = lines.reshape(count, BASIS_COUNT, 3 * WINDOW)
    lines = jnp.pad(lines, ((0, 0), (0, FILTER_ROWS - BASIS_COUNT), (0, 256 - 3 * WINDOW)))
    return lines.reshape(count * FILTER_ROWS, 256)


def on_device(
    grid_inputs,
    stencil_prenorm_scale,
    patch_kernel_profiles,
    channel_mixer_tensor,
    softmax_prenorm_scale,
    probe_lookup_content_projector,
    head_logit_scales,
    final_projector,
    azimuth_reaches,
):
    rows, longitudes, channels = grid_inputs.shape
    assert rows >= HALO and longitudes % BAND == 0 and channels == 256
    flat = grid_inputs.reshape(rows * longitudes, channels)
    lines = filter_lines(patch_kernel_profiles, azimuth_reaches, False)
    flipped = filter_lines(patch_kernel_profiles, azimuth_reaches, True)
    local = jnp.concatenate([flat, lines], axis=0)
    if rows == HALO:
        upward = downward = local
    else:
        upward = jnp.concatenate([flat[-HALO * longitudes :], lines[-HALO * FILTER_ROWS :]], axis=0)
        downward = jnp.concatenate([flat[: HALO * longitudes], lines[: HALO * FILTER_ROWS]], axis=0)
    count = lax.axis_size("band")
    position = lax.axis_index("band")
    forward = [(i, i + 1) for i in range(count - 1)]
    backward = [(target, source) for source, target in forward]
    low = lax.ppermute(upward, "band", forward)
    high = lax.ppermute(downward, "band", backward)
    flags = jnp.stack([position == 0, position == count - 1]).astype(jnp.int32)
    wide = rows + 2 * PATCH_LAT_EXTENT
    smem = pl.BlockSpec(memory_space=pltpu.SMEM)
    vmem = pl.BlockSpec(memory_space=pltpu.VMEM)
    return pl.pallas_call(
        functools.partial(window_kernel, rows, longitudes),
        out_shape=jax.ShapeDtypeStruct(grid_inputs.shape, BF16),
        in_specs=[smem] * 3 + [vmem] * 9,
        out_specs=vmem,
        scratch_shapes=[
            pltpu.VMEM((rows + 2 * HALO, longitudes, channels), BF16),
            pltpu.VMEM((rows + 2 * HALO, longitudes + 32, channels), BF16),
            pltpu.VMEM((wide, FILTER_ROWS, channels), F32),
            pltpu.VMEM((BASIS_COUNT * BAND, channels), BF16),
            pltpu.VMEM((longitudes, BASIS_COUNT * channels), BF16),
            pltpu.VMEM((wide, longitudes, channels), F32),
            pltpu.VMEM((wide, longitudes, channels), BF16),
            pltpu.VMEM((wide, longitudes + 2 * DISC_REACH, channels), BF16),
            pltpu.VMEM((wide, longitudes + 2 * DISC_REACH, channels), BF16),
            pltpu.VMEM((rows, longitudes, channels), BF16),
            pltpu.VMEM((rows, DISC_ROWS * KEYS, HEAD_COUNT * QUERIES), F32),
            pltpu.VMEM((rows, longitudes, channels), BF16),
        ],
        compiler_params=pltpu.CompilerParams(vmem_limit_bytes=56 * 1024 * 1024),
    )(
        flags,
        azimuth_reaches,
        head_logit_scales,
        local,
        low,
        high,
        flipped,
        stencil_prenorm_scale.reshape(1, channels),
        channel_mixer_tensor,
        softmax_prenorm_scale.reshape(1, channels),
        probe_lookup_content_projector,
        final_projector,
    )


def solution(mesh):
    placed = (
        P(("members", "band"), None, None),
        P(),
        P("band", None, None),
        P(),
        P(),
        P(),
        P(),
        P(),
        P("band", None),
    )
    return jax.shard_map(
        on_device,
        mesh=mesh,
        in_specs=placed,
        out_specs=P(("members", "band"), None, None),
        check_vma=False,
    )
```

time: 212 us -> 62.8 us (0.30); the launches traced: 209 us -> 61.7 us
  local copies, waits for them, and re-layouts: 67.7 us -> 3.69 us
  matrix products: 59.8 us -> 0 us
  other arithmetic: 46.4 us -> 1.85 us
  Pallas kernels: 0 us -> 39.5 us
  loops' own time: 19.8 us -> 0 us
  waiting for transfers between devices: 4.58 us -> 10.9 us
  starting transfers between devices: 9.93 us -> 5.63 us
    dot_general x15 -> x0, matrix products: 59.8 us -> none  [the longest x3 22.1 us: conv_row(): jnp.einsum('kt,tjc->jkc', filters[present_parallel_number], tap_stack, pr...]
    pallas_call x0 -> x1, Pallas kernels: none -> 39.5 us  [on_device(): pl.pallas_call(functools.partial(window_kernel, rows, longitudes), out_sh...]
    while x21 -> x0, other arithmetic: 23 us -> none
    another operation x2 -> x0, loops' own time: 19.8 us -> none  [the longest x1 11 us: on_device(): mixture = lax.map(attend_local, jnp.arange(row_count, dtype=jnp.int32))]
    concatenate x6 -> x0, local copies, waits for them, and re-layouts: 17.7 us -> none  [lon_windows(): jnp.concatenate([blocks[:, :-1], blocks[:, 1:, :2 * DISC_REACH]], axis=2)]
    convert_element_type x7 -> x0, local copies, waits for them, and re-layouts: 13.6 us -> none  [the longest x3 11.5 us: conv_row(): basis_sums = jnp.einsum('kt,tjc->jkc', filters[present_parallel_number],...]
    reduce_sum x7 -> x0, other arithmetic: 10.3 us -> none  [the longest x3 6.54 us: look_at_one_parallel(): jnp.sum(exponent, axis=-1, keepdims=True)]
    slice x58 -> x1, local copies, waits for them, and re-layouts: 10.3 us -> 0.75 us  [filter_lines(): limits = reaches[:, PATCH_LAT_EXTENT - 1:PATCH_LAT_EXTENT + 2]]
  transfers between devices with their start and end apart: 4 -> 2, of which waited for: 2 -> 1; matrix products, arithmetic and copies ran while one was open for 5% -> 2% of each run, Pallas kernels for 0% -> 0%
where the time goes in v1:
time: 62.8 us; the launch traced here: 61.7 us
  Pallas kernels  39.5 us (63%)
  waiting for transfers between devices  10.9 us (17%)
  starting transfers between devices  5.63 us (9%)
  local copies, waits for them, and re-layouts  3.69 us (6%)
  other arithmetic  1.85 us (3%)
    pallas_call x1, Pallas kernels, on_device(): pl.pallas_call(functools.partial(window_kernel, rows, longitudes), out_sh...  39.5 us
    ppermute x1, waiting for transfers between devices, on_device(): high = lax.ppermute(downward, 'band', backward)  10.9 us
    ppermute x1, starting transfers between devices, on_device(): low = lax.ppermute(upward, 'band', forward)  3.05 us
    ppermute x1, starting transfers between devices, on_device(): high = lax.ppermute(downward, 'band', backward)  2.58 us
  transfers between devices with their start and end apart: 2, of which 1 were waited for; matrix products, arithmetic and copies ran while one was open for 2% of the time, Pallas kernels for 0%

profile of v1, /device:TPU:25, one launch (start us, length us, event | category | flops | bytes accessed | tf_op | source)
XLA Modules:
  0.0 61.7 jit_solution(6682173513773338835)
XLA Ops:
  0.0 0.8 %slice.4 = s32[3,3]{1,0:T(4,128)S(1)} slice(s32[3,5]{1,0:T(4,128)} %reaches.1), slice={[0:3], [1:4]} | slice | bytes 72 | tf_op jit(solution)/shard_map/slice | solution.py:243
  0.8 0.8 %reshape.33 = bf16[3,9,3,9]{3,2,0,1:T(4,128)(2,1)S(1)} reshape(f32[3,9,27]{2,0,1:T(4,128)} %param.11) | data formatting | bytes 4374 | tf_op jit(solution)/shard_map/reshape | solution.py:245
  1.6 0.1 broadcast_compare_fusion
  1.7 0.1 pad.14
  1.8 0.1 reshape.34
  1.9 1.1 %pad_maximum_fusion.local = bf16[1200,256]{1,0:T(8,128)(2,1)S(1)} fusion(bf16[48,256]{1,0:T(8,128)(2,1)S(1)} %bitcast.15, bf16[1152,256]{1,0:T(8,128)(2,1)} %bitcast.13), kind=kLoop, calls=%fused_computation | loop fusion | flops 1228800 | bytes 1228800 | tf_op jit(solution)/shard_map/concatenate | solution.py:272
  3.0 0.0 copy-start
  3.0 2.6 %collective-permute-start.1 = (bf16[1200,256]{1,0:T(8,128)(2,1)S(1)}, bf16[1200,256]{1,0:T(8,128)(2,1)S(1)}, u32[]{:S(2)}, u32[]{:S(2)}) collective-permute-start(bf16[1200,256]{1,0:T(8,128)(2,1)S(1)} %pad_maximum_fusion.local), channel_id=1, source_target_pairs={{1,0},{2,1},{3,2},{4,3},{5,4},{6,5},{7,6},{8,7},{9,8},{10,9},{11,1... | collective-permute-start | bytes 1843208 | tf_op jit(solution)/shard_map/ppermute | solution.py:283
  5.6 3.0 %collective-permute-start = (bf16[1200,256]{1,0:T(8,128)(2,1)S(1)}, bf16[1200,256]{1,0:T(8,128)(2,1)S(1)}, u32[]{:S(2)}, u32[]{:S(2)}) collective-permute-start(bf16[1200,256]{1,0:T(8,128)(2,1)S(1)} %pad_maximum_fusion.local), channel_id=1, source_target_pairs={{0,1},{1,2},{2,3},{3,4},{4,5},{5,6},{6,7},{7,8},{8,9},{9,10},{10,1... | collective-permute-start | bytes 1843208 | tf_op jit(solution)/shard_map/ppermute | solution.py:282
  8.7 0.1 rev.3
  8.7 0.1 pad.16
  8.8 0.1 reshape.36
  8.9 0.6 %pad.17.clone = bf16[3,16,256]{2,1,0:T(8,128)(2,1)} pad(bf16[3,9,240]{2,1,0:T(8,128)(2,1)S(1)} %copy.15, bf16[]{:T(256)} %constant.14.clone.1), padding=0_0x0_7x0_16 | pad | bytes 37538 | tf_op jit(solution)/shard_map/jit(_pad)/pad | solution.py:252
  9.6 0.6 %add_convert_fusion.flags = s32[2]{0:T(128)} fusion(pred[1]{0:T(512)(128)(4,1)} %bitcast.1, pred[1]{0:T(512)(128)(4,1)} %bitcast), kind=kLoop, calls=%fused_computation.3 | loop fusion | flops 4 | bytes 10 | tf_op jit(solution)/shard_map/convert_element_type | solution.py:284
  10.2 10.9 %collective-permute-done.1.high = bf16[1200,256]{1,0:T(8,128)(2,1)S(1)} collective-permute-done((bf16[1200,256]{1,0:T(8,128)(2,1)S(1)}, bf16[1200,256]{1,0:T(8,128)(2,1)S(1)}, u32[]{:S(2)}, u32[]{:S(2)}) %collective-permute-start.1) | collective-permute-done | bytes 614432 | tf_op jit(solution)/shard_map/ppermute | solution.py:283
  21.1 0.0 copy-start.1
  21.1 0.0 collective-permute-done.low
  21.1 0.0 copy-start.2
  21.1 0.0 copy-done
  21.1 0.8 %copy-done.1 = bf16[1200,256]{1,0:T(8,128)(2,1)} copy-done((bf16[1200,256]{1,0:T(8,128)(2,1)}, bf16[1200,256]{1,0:T(8,128)(2,1)S(1)}, u32[]{:S(2)}) %copy-start.1) | copy-done | bytes 614424
  22.0 0.2 copy-done.2
  22.2 39.5 %shard_map.91 = bf16[3,384,256]{2,1,0:T(8,128)(2,1)} custom-call(s32[2]{0:T(128)} %add_convert_fusion.flags, s32[3,5]{1,0:T(4,128)} %reaches.1, f32[8]{0:T(128)} %scales.1, bf16[1200,256]{1,0:T(8,128)(2,1)} %copy-done, bf16[1200,256]{1,0:T(8,128)(2,1)} %copy-done.2, bf16[1200,256]{1,0:T(8,128)(2,1)} %copy-done.1, bf16[48,256]{1,0:T(8,128)(2,1)} %bitcast.14, ...), custom_call_target="tpu_custom_call" | custom-call | tf_op jit(solution)/shard_map/pallas_call | solution.py:288
  (5 shorter events, 0.0 us)
Async XLA Ops:
  3.0 18.1 %copy-start = (bf16[1200,256]{1,0:T(8,128)(2,1)}, bf16[1200,256]{1,0:T(8,128)(2,1)S(1)}, u32[]{:S(2)}) copy-start(bf16[1200,256]{1,0:T(8,128)(2,1)S(1)} %pad_maximum_fusion.local) | copy-start | bytes 1843204
  3.0 18.1 %collective-permute-start.1 = (bf16[1200,256]{1,0:T(8,128)(2,1)S(1)}, bf16[1200,256]{1,0:T(8,128)(2,1)S(1)}, u32[]{:S(2)}, u32[]{:S(2)}) collective-permute-start(bf16[1200,256]{1,0:T(8,128)(2,1)S(1)} %pad_maximum_fusion.local), channel_id=1, source_target_pairs={{1,0},{2,1},{3,2},{4,3},{5,4},{6,5},{7,6},{8,7},{9,8},{10,9},{11,1... | collective-permute-start | bytes 1843208 | tf_op jit(solution)/shard_map/ppermute | solution.py:283
  5.6 15.5 %collective-permute-start = (bf16[1200,256]{1,0:T(8,128)(2,1)S(1)}, bf16[1200,256]{1,0:T(8,128)(2,1)S(1)}, u32[]{:S(2)}, u32[]{:S(2)}) collective-permute-start(bf16[1200,256]{1,0:T(8,128)(2,1)S(1)} %pad_maximum_fusion.local), channel_id=1, source_target_pairs={{0,1},{1,2},{2,3},{3,4},{4,5},{5,6},{6,7},{7,8},{8,9},{9,10},{10,1... | collective-permute-start | bytes 1843208 | tf_op jit(solution)/shard_map/ppermute | solution.py:282
  21.1 0.8 %copy-start.1 = (bf16[1200,256]{1,0:T(8,128)(2,1)}, bf16[1200,256]{1,0:T(8,128)(2,1)S(1)}, u32[]{:S(2)}) copy-start(bf16[1200,256]{1,0:T(8,128)(2,1)S(1)} %collective-permute-done.1.high) | copy-start | bytes 1843204
  21.1 1.0 %copy-start.2 = (bf16[1200,256]{1,0:T(8,128)(2,1)}, bf16[1200,256]{1,0:T(8,128)(2,1)S(1)}, u32[]{:S(2)}) copy-start(bf16[1200,256]{1,0:T(8,128)(2,1)S(1)} %collective-permute-done.low) | copy-start | bytes 1843204

commit v2 on v1

v2 whole, which is shorter than its diff:
```python
import functools

import jax
import jax.numpy as jnp
from jax import lax
from jax.experimental import pallas as pl
from jax.experimental.pallas import tpu as pltpu
from jax.sharding import PartitionSpec as P

HEAD_COUNT = 8
HEAD_WIDTH = 32
BASIS_COUNT = 9
CONV_REACH = 4
PATCH_LAT_EXTENT = 2
DISC_REACH = 8
TAPS = 2 * CONV_REACH + 1
DISC_ROWS = 2 * PATCH_LAT_EXTENT + 1
EPSILON = 1e-06
HALO = PATCH_LAT_EXTENT + 1
BAND = 64
WINDOW = BAND + 16
QUERIES = 16
KEYS = QUERIES + 2 * DISC_REACH
FILTER_ROWS = 16
F32 = jnp.float32
BF16 = jnp.bfloat16


def scaled_norm(values, gain):
    inverse = lax.rsqrt(jnp.mean(values * values, axis=-1, keepdims=True) + EPSILON)
    return values * inverse * gain


def head_unit(values, ones):
    squares = values * values
    high = squares.astype(BF16)
    low = (squares - high.astype(F32)).astype(BF16)
    total = jnp.dot(high, ones, preferred_element_type=F32) + jnp.dot(
        low, ones, preferred_element_type=F32
    )
    return values * lax.rsqrt(total + EPSILON)


def wrapped(values, before, after):
    parts = [values[values.shape[0] - before :], values, values[:after]]
    return jnp.concatenate(parts, axis=0)


def band_rows(filters, row, bands):
    channels = filters.shape[-1]
    for k in range(BASIS_COUNT):
        line = jnp.broadcast_to(filters[row, k : k + 1, :], (BAND, channels))
        line = pltpu.roll(line, 0, 1, stride=1, stride_axis=0)
        bands[k * BAND : (k + 1) * BAND, :] = line.astype(BF16)


def conv_row(row, raw, normed, filters, mixer, bands, basis, shift):
    longitudes, channels = raw.shape[1:]
    band_rows(filters, row + shift, bands)
    for block in range(longitudes // BAND):
        start = block * BAND
        window = jnp.concatenate(
            [
                normed[row, start : start + WINDOW, :],
                normed[row + 1, start : start + WINDOW, :],
                normed[row + 2, start : start + WINDOW + 16, :],
            ],
            axis=0,
        )
        sums = jnp.dot(bands[...], window, preferred_element_type=F32).astype(BF16)
        for k in range(BASIS_COUNT):
            basis[start : start + BAND, k * channels : (k + 1) * channels] = sums[
                k * BAND : (k + 1) * BAND
            ]
    return raw[row + 1].astype(F32) + jnp.dot(
        basis[...], mixer[...], preferred_element_type=F32
    )


def norm_rows(count, raw, normed, gain):
    def norm_row(row, carry):
        block = scaled_norm(raw[row].astype(F32), gain[...])
        normed[row] = wrapped(block, 8, 24).astype(BF16)
        return carry

    lax.fori_loop(0, count, norm_row, 0)


def head_ones(channels):
    head_of_lane = lax.broadcasted_iota(jnp.int32, (channels, channels), 1) // HEAD_WIDTH
    head_of_row = lax.broadcasted_iota(jnp.int32, (channels, channels), 0) // HEAD_WIDTH
    return jnp.where(head_of_lane == head_of_row, 1.0, 0.0).astype(BF16)


def key_row(block, projector, ones):
    channels = block.shape[1]
    both = jnp.dot(block, projector[:, channels : 3 * channels], preferred_element_type=F32)
    rounded = both.astype(BF16).astype(F32)
    unit = head_unit(rounded[:, :channels], ones)
    return (
        wrapped(unit, DISC_REACH, DISC_REACH).astype(BF16),
        wrapped(rounded[:, channels:], DISC_REACH, DISC_REACH).astype(BF16),
    )


def query_row(block, projector, ones):
    channels = block.shape[1]
    probe = jnp.dot(block, projector[:, :channels], preferred_element_type=F32)
    return head_unit(probe.astype(BF16).astype(F32), ones).astype(BF16)


def lines_kernel(rows, reaches, profiles, source, payload, flipped, pad):
    size = source.shape[0]
    payload[:size, :] = source[...]
    shape = (FILTER_ROWS, pad.shape[1])
    lane = lax.broadcasted_iota(jnp.int32, shape, 1)
    for row in range(rows):
        pad[...] = jnp.zeros(shape, F32)
        pad[:BASIS_COUNT, : 3 * TAPS] = profiles[row]
        block = pad[...]
        straight = jnp.zeros(shape, F32)
        mirrored = jnp.zeros(shape, F32)
        for a in range(3):
            distance = jnp.abs(lane - (a * TAPS + CONV_REACH))
            seen = distance <= jnp.minimum(reaches[row, PATCH_LAT_EXTENT - 1 + a], CONV_REACH)
            part = jnp.where(seen, block, 0.0)
            shift = a * WINDOW + CONV_REACH - a * TAPS
            straight = straight + pltpu.roll(part, shift, 1)
            shift = (2 - a) * WINDOW + CONV_REACH - a * TAPS
            mirrored = mirrored + pltpu.roll(part, shift % pad.shape[1], 1)
        base = row * FILTER_ROWS
        payload[size + base : size + base + FILTER_ROWS, :] = straight.astype(BF16)
        flipped[base : base + FILTER_ROWS, :] = mirrored.astype(BF16)


def near_kernel(
    rows,
    longitudes,
    flags,
    local,
    partner,
    conv_gain,
    mixer,
    attn_gain,
    projector,
    hidden,
    keys,
    values,
    queries,
    raw,
    normed,
    filters,
    bands,
    basis,
):
    channels = local.shape[1]
    even = flags[2]
    mine = (1 - even) * HALO
    other = HALO - mine
    for row in range(HALO):
        at = row * longitudes
        raw[mine + row] = local[at : at + longitudes, :]
        raw[other + row] = partner[at : at + longitudes, :]
        at = HALO * longitudes + row * FILTER_ROWS
        filters[mine + row] = local[at : at + FILTER_ROWS, :].astype(F32)
        filters[other + row] = partner[at : at + FILTER_ROWS, :].astype(F32)
    norm_rows(2 * HALO, raw, normed, conv_gain)
    ones = head_ones(channels)

    def conv_step(row, carry):
        total = conv_row(row, raw, normed, filters, mixer, bands, basis, 1)
        hidden[row] = total
        block = scaled_norm(total, attn_gain[...]).astype(BF16)
        keys[row], values[row] = key_row(block, projector, ones)
        queries[row] = query_row(block, projector, ones)
        return carry

    lax.fori_loop(0, 2 * HALO - 2, conv_step, 0)


def far_kernel(
    rows,
    longitudes,
    flags,
    reaches,
    scales,
    local,
    cross,
    cross_lines,
    flipped,
    conv_gain,
    mixer,
    attn_gain,
    projector,
    final,
    near_hidden,
    near_keys,
    near_values,
    near_queries,
    out,
    raw,
    normed,
    filters,
    bands,
    basis,
    hidden,
    keys,
    values,
    queries,
    bias,
    mixture,
):
    channels = local.shape[1]
    half = longitudes // 2
    pole = flags[0] + flags[1] > 0
    even = flags[2]
    wide = rows + 2 * PATCH_LAT_EXTENT
    near = 2 * HALO - 2
    far = wide - near

    def local_row(row):
        return local[row * longitudes : (row + 1) * longitudes, :]

    def rolled(row):
        block = local_row(row)
        return jnp.concatenate([block[half:], block[:half]], axis=0)

    far_base = (1 - even) * 2
    for step in range(HALO):
        there = cross[step * longitudes : (step + 1) * longitudes, :]
        raw[far_base + step] = jnp.where(pole, rolled(HALO - 1 - step), there)
    own_base = even * HALO
    for step in range(2):
        lower, upper = local_row(step), local_row(step + 1)
        raw[own_base + step] = jnp.where(even > 0, lower, upper)

    def lines(ref, row):
        return ref[row * FILTER_ROWS : (row + 1) * FILTER_ROWS, :].astype(F32)

    base = rows * longitudes // FILTER_ROWS
    for u in range(far):
        from_even = lines(local, base) if u == far - 1 else jnp.where(
            pole, lines(flipped, far - 2 - u), lines(cross_lines, u + 1)
        )
        from_odd = lines(local, base + rows - 1) if u == 0 else jnp.where(
            pole, lines(flipped, rows - u), lines(cross_lines, u - 1)
        )
        filters[u] = jnp.where(even > 0, from_even, from_odd)
    norm_rows(far + 2, raw, normed, conv_gain)
    ones = head_ones(channels)
    far_slot = (1 - even) * near
    near_slot = even * far

    def copy_near(row, carry):
        hidden[near_slot + row] = near_hidden[row]
        keys[near_slot + row] = near_keys[row]
        values[near_slot + row] = near_values[row]
        queries[near_slot + row] = near_queries[row]
        return carry

    lax.fori_loop(0, near, copy_near, 0)

    def conv_step(row, carry):
        total = conv_row(row, raw, normed, filters, mixer, bands, basis, 0)
        slot = far_slot + row
        hidden[slot] = total
        block = scaled_norm(total, attn_gain[...]).astype(BF16)
        keys[slot], values[slot] = key_row(block, projector, ones)
        queries[slot] = query_row(block, projector, ones)
        return carry

    lax.fori_loop(0, far, conv_step, 0)

    lanes = HEAD_COUNT * QUERIES

    def bias_row(row, carry):
        key_at = lax.broadcasted_iota(jnp.int32, (KEYS, lanes), 0)
        query_at = lax.broadcasted_iota(jnp.int32, (KEYS, lanes), 1) % QUERIES
        distance = jnp.abs(key_at - DISC_REACH - query_at)
        for a in range(DISC_ROWS):
            bias[row, a * KEYS : (a + 1) * KEYS, :] = jnp.where(
                distance <= reaches[row, a], 0.0, -1e30
            ).astype(F32)
        return carry

    lax.fori_loop(0, rows, bias_row, 0)

    lane_head = lax.broadcasted_iota(jnp.int32, (1, lanes), 1) // QUERIES
    scale = jnp.zeros((1, lanes), F32)
    for h in range(HEAD_COUNT):
        scale = jnp.where(lane_head == h, scales[h], scale)
    channel_head = lax.broadcasted_iota(jnp.int32, (QUERIES, channels), 1) // HEAD_WIDTH

    unroll = 4
    per_row = longitudes // (QUERIES * unroll)

    def attend(step, carry):
        row = step // per_row
        base = (step % per_row) * (QUERIES * unroll)
        for u in range(unroll):
            start = pl.multiple_of(base + u * QUERIES, QUERIES)
            probe = queries[row + PATCH_LAT_EXTENT, pl.ds(start, QUERIES), :]
            spread = jnp.concatenate(
                [jnp.where(channel_head == h, probe, jnp.zeros_like(probe)) for h in range(HEAD_COUNT)],
                axis=0,
            )
            near_k = jnp.concatenate(
                [keys[row + a, pl.ds(start, KEYS), :] for a in range(DISC_ROWS)], axis=0
            )
            near_v = jnp.concatenate(
                [values[row + a, pl.ds(start, KEYS), :] for a in range(DISC_ROWS)], axis=0
            )
            scores = lax.dot_general(
                near_k, spread, (((1,), (1,)), ((), ())), preferred_element_type=F32
            )
            scores = scores + bias[row]
            peak = jnp.max(scores, axis=0, keepdims=True)
            weights = jnp.exp((scores - peak) * scale)
            total = jnp.sum(weights, axis=0, keepdims=True)
            weights = (weights * (1.0 / total)).astype(BF16)
            mixed = lax.dot_general(
                weights, near_v, (((0,), (0,)), ((), ())), preferred_element_type=F32
            )
            result = jnp.zeros((QUERIES, channels), F32)
            for h in range(HEAD_COUNT):
                result = jnp.where(
                    channel_head == h, mixed[h * QUERIES : (h + 1) * QUERIES], result
                )
            mixture[row, pl.ds(start, QUERIES), :] = result.astype(BF16)
        return carry

    lax.fori_loop(0, rows * per_row, attend, 0)

    def finish(row, carry):
        product = jnp.dot(mixture[row], final[...], preferred_element_type=F32)
        out[row] = (hidden[row + PATCH_LAT_EXTENT] + product).astype(BF16)
        return carry

    lax.fori_loop(0, rows, finish, 0)


def on_device(
    grid_inputs,
    stencil_prenorm_scale,
    patch_kernel_profiles,
    channel_mixer_tensor,
    softmax_prenorm_scale,
    probe_lookup_content_projector,
    head_logit_scales,
    final_projector,
    azimuth_reaches,
):
    rows, longitudes, channels = grid_inputs.shape
    count = lax.axis_size("band")
    assert rows == HALO and longitudes % BAND == 0 and channels == 256 and count % 2 == 0
    position = lax.axis_index("band")
    within = [(i, i ^ 1) for i in range(count)]
    across = [pair for i in range(1, count - 1, 2) for pair in ((i, i + 1), (i + 1, i))]
    flat = grid_inputs.reshape(rows * longitudes, channels)
    cross = lax.ppermute(flat, "band", across)
    smem = pl.BlockSpec(memory_space=pltpu.SMEM)
    vmem = pl.BlockSpec(memory_space=pltpu.VMEM)
    limit = pltpu.CompilerParams(vmem_limit_bytes=48 * 1024 * 1024)
    size = rows * longitudes
    local, flipped = pl.pallas_call(
        functools.partial(lines_kernel, rows),
        out_shape=(
            jax.ShapeDtypeStruct((size + rows * FILTER_ROWS, channels), BF16),
            jax.ShapeDtypeStruct((rows * FILTER_ROWS, channels), BF16),
        ),
        in_specs=[smem, vmem, vmem],
        out_specs=(vmem, vmem),
        scratch_shapes=[pltpu.VMEM((FILTER_ROWS, channels), F32)],
    )(azimuth_reaches, patch_kernel_profiles, flat)
    partner = lax.ppermute(local, "band", within)
    cross_lines = lax.ppermute(local[size:], "band", across)
    flags = jnp.stack([position == 0, position == count - 1, position % 2 == 0]).astype(jnp.int32)
    conv_gain = stencil_prenorm_scale.reshape(1, channels)
    attn_gain = softmax_prenorm_scale.reshape(1, channels)
    near = 2 * HALO - 2
    wide = rows + 2 * PATCH_LAT_EXTENT
    padded = longitudes + 2 * DISC_REACH
    shared = [
        pltpu.VMEM((BASIS_COUNT * BAND, channels), BF16),
        pltpu.VMEM((longitudes, BASIS_COUNT * channels), BF16),
    ]
    near_state = pl.pallas_call(
        functools.partial(near_kernel, rows, longitudes),
        out_shape=(
            jax.ShapeDtypeStruct((near, longitudes, channels), F32),
            jax.ShapeDtypeStruct((near, padded, channels), BF16),
            jax.ShapeDtypeStruct((near, padded, channels), BF16),
            jax.ShapeDtypeStruct((near, longitudes, channels), BF16),
        ),
        in_specs=[smem] + [vmem] * 6,
        out_specs=(vmem,) * 4,
        scratch_shapes=[
            pltpu.VMEM((2 * HALO, longitudes, channels), BF16),
            pltpu.VMEM((2 * HALO, longitudes + 32, channels), BF16),
            pltpu.VMEM((2 * HALO, FILTER_ROWS, channels), F32),
        ]
        + shared,
        compiler_params=limit,
        cost_estimate=pl.CostEstimate(flops=8 * 10**9, bytes_accessed=8 * 10**6, transcendentals=0),
    )(flags, local, partner, conv_gain, channel_mixer_tensor, attn_gain, probe_lookup_content_projector)
    return pl.pallas_call(
        functools.partial(far_kernel, rows, longitudes),
        out_shape=jax.ShapeDtypeStruct(grid_inputs.shape, BF16),
        in_specs=[smem] * 3 + [vmem] * 13,
        out_specs=vmem,
        scratch_shapes=[
            pltpu.VMEM((HALO + 2, longitudes, channels), BF16),
            pltpu.VMEM((HALO + 2, longitudes + 32, channels), BF16),
            pltpu.VMEM((HALO, FILTER_ROWS, channels), F32),
        ]
        + shared
        + [
            pltpu.VMEM((wide, longitudes, channels), F32),
            pltpu.VMEM((wide, padded, channels), BF16),
            pltpu.VMEM((wide, padded, channels), BF16),
            pltpu.VMEM((wide, longitudes, channels), BF16),
            pltpu.VMEM((rows, DISC_ROWS * KEYS, HEAD_COUNT * QUERIES), F32),
            pltpu.VMEM((rows, longitudes, channels), BF16),
        ],
        compiler_params=limit,
        cost_estimate=pl.CostEstimate(flops=10**10, bytes_accessed=8 * 10**6, transcendentals=10**6),
    )(
        flags,
        azimuth_reaches,
        head_logit_scales,
        local,
        cross,
        cross_lines,
        flipped,
        conv_gain,
        channel_mixer_tensor,
        attn_gain,
        probe_lookup_content_projector,
        final_projector,
        *near_state,
    )


def solution(mesh):
    placed = (
        P(("members", "band"), None, None),
        P(),
        P("band", None, None),
        P(),
        P(),
        P(),
        P(),
        P(),
        P("band", None),
    )
    return jax.shard_map(
        on_device,
        mesh=mesh,
        in_specs=placed,
        out_specs=P(("members", "band"), None, None),
        check_vma=False,
    )
```

time: 62.8 us -> 55.2 us (0.88)
  the two profiles are of different devices: /device:TPU:25 before, /device:TPU:5 now
where the time goes in v2:
time: 55.2 us; the launch traced here: 54.8 us
  Pallas kernels  40.7 us (74%)
  starting transfers between devices  7.11 us (13%)
  local copies, waits for them, and re-layouts  6.8 us (12%)
    pallas_call x1, Pallas kernels, on_device(): pl.pallas_call(functools.partial(far_kernel, rows, longitudes), out_shape...  26.8 us
    pallas_call x1, Pallas kernels, on_device(): pl.pallas_call(functools.partial(near_kernel, rows, longitudes), out_shap...  11.8 us
    unnamed x23, local copies, waits for them, and re-layouts  6.05 us
    ppermute x1, starting transfers between devices, on_device(): cross_lines = lax.ppermute(local[size:], 'band', across)  3.41 us
    ppermute x1, starting transfers between devices, on_device(): cross = lax.ppermute(flat, 'band', across)  3.03 us
    pallas_call x1, Pallas kernels, on_device(): pl.pallas_call(functools.partial(lines_kernel, rows), out_shape=(jax.Shap...  2.06 us
  transfers between devices with their start and end apart: 3, of which 0 were waited for; matrix products, arithmetic and copies ran while one was open for 1% of the time, Pallas kernels for 21%

profile of v2, /device:TPU:5, one launch (start us, length us, event | category | flops | bytes accessed | tf_op | source)
XLA Modules:
  0.0 54.8 jit_solution(10448983486727712398)
XLA Ops:
  0.0 1.3 %copy.10.profiles = f32[3,9,27]{2,1,0:T(8,128)} copy(f32[3,9,27]{2,0,1:T(4,128)} %param.11) | data formatting | bytes 5832 | tf_op args[2]
  1.3 2.1 %shard_map.91 = (bf16[1200,256]{1,0:T(8,128)(2,1)}, bf16[48,256]{1,0:T(8,128)(2,1)}) custom-call(s32[3,5]{1,0:T(4,128)} %reaches.3, f32[3,9,27]{2,1,0:T(8,128)} %copy.10.profiles, bf16[1152,256]{1,0:T(8,128)(2,1)} %bitcast.10), custom_call_target="tpu_custom_call" | custom-call | tf_op jit(solution)/shard_map/pallas_call | solution.py:365
  3.4 0.7 %collective-permute-start.2 = (bf16[1200,256]{1,0:T(8,128)(2,1)}, bf16[1200,256]{1,0:T(8,128)(2,1)S(1)}, u32[]{:S(2)}, u32[]{:S(2)}) collective-permute-start(bf16[1200,256]{1,0:T(8,128)(2,1)} %get-tuple-element.11.local), channel_id=1, source_target_pairs={{0,1},{1,0},{2,3},{3,2},{4,5},{5,4},{6,7},{7,6},{8,9},{9,8},{10,11... | collective-permute-start | bytes 1843208 | tf_op jit(solution)/shard_map/ppermute | solution.py:375
  4.1 3.0 %collective-permute-start = (bf16[1152,256]{1,0:T(8,128)(2,1)}, bf16[1152,256]{1,0:T(8,128)(2,1)S(1)}, u32[]{:S(2)}, u32[]{:S(2)}) collective-permute-start(bf16[1152,256]{1,0:T(8,128)(2,1)} %bitcast.11), channel_id=1, source_target_pairs={{1,2},{2,1},{3,4},{4,3},{5,6},{6,5},{7,8},{8,7},{9,10},{10,9},{11,... | collective-permute-start | bytes 1769480 | tf_op jit(solution)/shard_map/ppermute | solution.py:360
  7.1 0.7 %slice.3 = bf16[48,256]{1,0:T(8,128)(2,1)S(1)} slice(bf16[1200,256]{1,0:T(8,128)(2,1)} %get-tuple-element.11.local), slice={[1152:1200], [0:256]} | slice | bytes 49152 | tf_op jit(solution)/shard_map/slice | solution.py:376
  7.8 3.4 %collective-permute-start.1 = (bf16[48,256]{1,0:T(8,128)(2,1)S(1)}, bf16[48,256]{1,0:T(8,128)(2,1)S(1)}, u32[]{:S(2)}, u32[]{:S(2)}) collective-permute-start(bf16[48,256]{1,0:T(8,128)(2,1)S(1)} %slice.3), channel_id=1, source_target_pairs={{1,2},{2,1},{3,4},{4,3},{5,6},{6,5},{7,8},{8,7},{9,10},{10,9},{11,... | collective-permute-start | bytes 73736 | tf_op jit(solution)/shard_map/ppermute | solution.py:376
  11.3 0.1 add_convert_fusion.flags
  11.4 0.0 collective-permute-done.2.partner
  11.4 0.0 copy-start.1
  11.4 1.1 %copy-done.1 = bf16[1200,256]{1,0:T(8,128)(2,1)S(1)} copy-done((bf16[1200,256]{1,0:T(8,128)(2,1)S(1)}, bf16[1200,256]{1,0:T(8,128)(2,1)}, u32[]{:S(2)}) %copy-start.1) | copy-done | bytes 614424
  12.4 0.0 copy-start.2
  12.4 1.3 %copy-done.2 = bf16[2304,256]{1,0:T(8,128)(2,1)S(1)} copy-done((bf16[2304,256]{1,0:T(8,128)(2,1)S(1)}, bf16[2304,256]{1,0:T(8,128)(2,1)}, u32[]{:S(2)}) %copy-start.2) | copy-done | bytes 1179672
  13.7 0.0 copy-start.4
  13.7 1.0 %copy-done.4 = bf16[256,768]{1,0:T(8,128)(2,1)S(1)} copy-done((bf16[256,768]{1,0:T(8,128)(2,1)S(1)}, bf16[256,768]{1,0:T(8,128)(2,1)}, u32[]{:S(2)}) %copy-start.4) | copy-done | bytes 393240
  14.7 0.0 copy-start.8
  14.7 0.7 %copy-done.8 = f32[256]{0:T(256)S(1)} copy-done((f32[256]{0:T(256)S(1)}, f32[256]{0:T(256)}, u32[]{:S(2)}) %copy-start.8) | copy-done | bytes 1048
  15.4 0.0 copy-start.9
  15.4 0.7 %copy-done.9 = f32[256]{0:T(256)S(1)} copy-done((f32[256]{0:T(256)S(1)}, f32[256]{0:T(256)}, u32[]{:S(2)}) %copy-start.9) | copy-done | bytes 1048
  16.1 0.0 copy-start
  16.1 0.0 copy-start.5
  16.1 0.0 copy-start.7
  16.1 0.0 copy-start.10
  16.1 11.8 %shard_map.92 = (f32[4,384,256]{2,1,0:T(8,128)}, bf16[4,400,256]{2,1,0:T(8,128)(2,1)S(1)}, bf16[4,400,256]{2,1,0:T(8,128)(2,1)S(1)}, bf16[4,384,256]{2,1,0:T(8,128)(2,1)S(1)}) custom-call(s32[3]{0:T(128)S(1)} %add_convert_fusion.flags, bf16[1200,256]{1,0:T(8,128)(2,1)S(1)} %copy-done.1, bf16[1200,256]{1,0:T(8,128)(2,1)S(1)} %collective-permute-done.2.partner, ...), custom_call_target="tpu_custom_call" | custom-call | flops 8000000000 | bytes 8000000 | tf_op jit(solution)/shard_map/pallas_call | solution.py:387
  27.9 0.0 collective-permute-done.1.cross_lines
  27.9 0.0 collective-permute-done.cross
  27.9 0.0 copy-done
  27.9 0.0 copy-done.3
  27.9 0.0 copy-done.5
  27.9 0.0 copy-done.6
  27.9 0.0 copy-done.7
  27.9 0.0 copy-done.10
  27.9 26.8 %shard_map.93 = bf16[3,384,256]{2,1,0:T(8,128)(2,1)} custom-call(s32[3]{0:T(128)S(1)} %add_convert_fusion.flags, s32[3,5]{1,0:T(4,128)S(1)} %copy-done, f32[8]{0:T(128)S(1)} %copy-done.10, bf16[1200,256]{1,0:T(8,128)(2,1)S(1)} %copy-done.1, bf16[1152,256]{1,0:T(8,128)(2,1)S(1)} %collective-permute-done.cross, ...), custom_call_target="tpu_custom_call" | custom-call | flops 10000000000 | bytes 8000000 | tf_op jit(solution)/shard_map/pallas_call | solution.py:406
  (2 shorter events, 0.0 us)
Async XLA Ops:
  3.4 8.0 %collective-permute-start.2 = (bf16[1200,256]{1,0:T(8,128)(2,1)}, bf16[1200,256]{1,0:T(8,128)(2,1)S(1)}, u32[]{:S(2)}, u32[]{:S(2)}) collective-permute-start(bf16[1200,256]{1,0:T(8,128)(2,1)} %get-tuple-element.11.local), channel_id=1, source_target_pairs={{0,1},{1,0},{2,3},{3,2},{4,5},{5,4},{6,7},{7,6},{8,9},{9,8},{10,11... | collective-permute-start | bytes 1843208 | tf_op jit(solution)/shard_map/ppermute | solution.py:375
  4.1 23.8 %collective-permute-start = (bf16[1152,256]{1,0:T(8,128)(2,1)}, bf16[1152,256]{1,0:T(8,128)(2,1)S(1)}, u32[]{:S(2)}, u32[]{:S(2)}) collective-permute-start(bf16[1152,256]{1,0:T(8,128)(2,1)} %bitcast.11), channel_id=1, source_target_pairs={{1,2},{2,1},{3,4},{4,3},{5,6},{6,5},{7,8},{8,7},{9,10},{10,9},{11,... | collective-permute-start | bytes 1769480 | tf_op jit(solution)/shard_map/ppermute | solution.py:360
  7.8 20.0 %collective-permute-start.1 = (bf16[48,256]{1,0:T(8,128)(2,1)S(1)}, bf16[48,256]{1,0:T(8,128)(2,1)S(1)}, u32[]{:S(2)}, u32[]{:S(2)}) collective-permute-start(bf16[48,256]{1,0:T(8,128)(2,1)S(1)} %slice.3), channel_id=1, source_target_pairs={{1,2},{2,1},{3,4},{4,3},{5,6},{6,5},{7,8},{8,7},{9,10},{10,9},{11,... | collective-permute-start | bytes 73736 | tf_op jit(solution)/shard_map/ppermute | solution.py:376
  11.4 1.1 %copy-start.1 = (bf16[1200,256]{1,0:T(8,128)(2,1)S(1)}, bf16[1200,256]{1,0:T(8,128)(2,1)}, u32[]{:S(2)}) copy-start(bf16[1200,256]{1,0:T(8,128)(2,1)} %get-tuple-element.11.local) | copy-start | bytes 1843204
  12.4 1.3 %copy-start.2 = (bf16[2304,256]{1,0:T(8,128)(2,1)S(1)}, bf16[2304,256]{1,0:T(8,128)(2,1)}, u32[]{:S(2)}) copy-start(bf16[2304,256]{1,0:T(8,128)(2,1)} %mixer.3) | copy-start | bytes 3538948
  13.7 1.0 %copy-start.4 = (bf16[256,768]{1,0:T(8,128)(2,1)S(1)}, bf16[256,768]{1,0:T(8,128)(2,1)}, u32[]{:S(2)}) copy-start(bf16[256,768]{1,0:T(8,128)(2,1)} %projector.3) | copy-start | bytes 1179652
  14.7 0.7 %copy-start.8 = (f32[256]{0:T(256)S(1)}, f32[256]{0:T(256)}, u32[]{:S(2)}) copy-start(f32[256]{0:T(256)} %param.10) | copy-start | bytes 3076
  15.4 0.7 %copy-start.9 = (f32[256]{0:T(256)S(1)}, f32[256]{0:T(256)}, u32[]{:S(2)}) copy-start(f32[256]{0:T(256)} %param.13) | copy-start | bytes 3076
  16.1 11.8 %copy-start = (s32[3,5]{1,0:T(4,128)S(1)}, s32[3,5]{1,0:T(4,128)}, u32[]{:S(2)}) copy-start(s32[3,5]{1,0:T(4,128)} %reaches.3) | copy-start | bytes 184
  16.1 11.8 %copy-start.3 = (bf16[2304,256]{1,0:T(8,128)(2,1)S(1)}, bf16[2304,256]{1,0:T(8,128)(2,1)}, u32[]{:S(2)}) copy-start(bf16[2304,256]{1,0:T(8,128)(2,1)} %mixer.3) | copy-start | bytes 3538948
  16.1 11.8 %copy-start.5 = (bf16[256,768]{1,0:T(8,128)(2,1)S(1)}, bf16[256,768]{1,0:T(8,128)(2,1)}, u32[]{:S(2)}) copy-start(bf16[256,768]{1,0:T(8,128)(2,1)} %projector.3) | copy-start | bytes 1179652
  16.1 11.8 %copy-start.6 = (bf16[256,256]{1,0:T(8,128)(2,1)S(1)}, bf16[256,256]{1,0:T(8,128)(2,1)}, u32[]{:S(2)}) copy-start(bf16[256,256]{1,0:T(8,128)(2,1)} %final.1) | copy-start | bytes 393220
  16.1 11.8 %copy-start.7 = (bf16[48,256]{1,0:T(8,128)(2,1)S(1)}, bf16[48,256]{1,0:T(8,128)(2,1)}, u32[]{:S(2)}) copy-start(bf16[48,256]{1,0:T(8,128)(2,1)} %get-tuple-element.12.flipped) | copy-start | bytes 73732
  16.1 11.8 %copy-start.10 = (f32[8]{0:T(128)S(1)}, f32[8]{0:T(128)}, u32[]{:S(2)}) copy-start(f32[8]{0:T(128)} %scales.1) | copy-start | bytes 100

commit v3 on v2

v3 whole, which is shorter than its diff:
```python
import functools

import jax
import jax.numpy as jnp
from jax import lax
from jax.experimental import pallas as pl
from jax.experimental.pallas import tpu as pltpu
from jax.sharding import PartitionSpec as P

HEAD_COUNT = 8
HEAD_WIDTH = 32
BASIS_COUNT = 9
CONV_REACH = 4
PATCH_LAT_EXTENT = 2
DISC_REACH = 8
TAPS = 2 * CONV_REACH + 1
DISC_ROWS = 2 * PATCH_LAT_EXTENT + 1
EPSILON = 1e-06
HALO = PATCH_LAT_EXTENT + 1
BAND = 64
WINDOW = BAND + 16
QUERIES = 16
KEYS = QUERIES + 2 * DISC_REACH
FILTER_ROWS = 16
UNROLL = 12
VMEM_LIMIT = 67043328
F32 = jnp.float32
BF16 = jnp.bfloat16


def scaled_norm(values, gain):
    inverse = lax.rsqrt(jnp.mean(values * values, axis=-1, keepdims=True) + EPSILON)
    return values * inverse * gain


def head_unit(values, ones):
    squares = values * values
    high = squares.astype(BF16)
    low = (squares - high.astype(F32)).astype(BF16)
    total = jnp.dot(high, ones, preferred_element_type=F32) + jnp.dot(
        low, ones, preferred_element_type=F32
    )
    return values * lax.rsqrt(total + EPSILON)


def wrapped(values, before, after):
    parts = [values[values.shape[0] - before :], values, values[:after]]
    return jnp.concatenate(parts, axis=0)


def band_rows(filters, row, bands):
    channels = filters.shape[-1]
    for k in range(BASIS_COUNT):
        line = jnp.broadcast_to(filters[row, k : k + 1, :], (BAND, channels))
        line = pltpu.roll(line, 0, 1, stride=1, stride_axis=0)
        bands[k * BAND : (k + 1) * BAND, :] = line.astype(BF16)


def band_row(row, line_row, normed, filters, bands, basis):
    longitudes, channels = basis.shape[0], filters.shape[-1]
    band_rows(filters, line_row, bands)
    for block in range(longitudes // BAND):
        start = block * BAND
        window = jnp.concatenate(
            [
                normed[row, start : start + WINDOW, :],
                normed[row + 1, start : start + WINDOW, :],
                normed[row + 2, start : start + WINDOW + 16, :],
            ],
            axis=0,
        )
        sums = jnp.dot(bands[...], window, preferred_element_type=F32).astype(BF16)
        for k in range(BASIS_COUNT):
            basis[start : start + BAND, k * channels : (k + 1) * channels] = sums[
                k * BAND : (k + 1) * BAND
            ]


def mix_row(block, basis, mixer):
    return block.astype(F32) + jnp.dot(basis[...], mixer[...], preferred_element_type=F32)


def norm_rows(count, raw, normed, gain):
    def norm_row(row, carry):
        block = scaled_norm(raw[row].astype(F32), gain[...])
        normed[row] = wrapped(block, 8, 24).astype(BF16)
        return carry

    lax.fori_loop(0, count, norm_row, 0)


def head_ones(channels):
    head_of_lane = lax.broadcasted_iota(jnp.int32, (channels, channels), 1) // HEAD_WIDTH
    head_of_row = lax.broadcasted_iota(jnp.int32, (channels, channels), 0) // HEAD_WIDTH
    return jnp.where(head_of_lane == head_of_row, 1.0, 0.0).astype(BF16)


def key_row(block, projector, ones):
    channels = block.shape[1]
    both = jnp.dot(block, projector[:, channels : 3 * channels], preferred_element_type=F32)
    rounded = both.astype(BF16).astype(F32)
    unit = head_unit(rounded[:, :channels], ones)
    return (
        wrapped(unit, DISC_REACH, DISC_REACH).astype(BF16),
        wrapped(rounded[:, channels:], DISC_REACH, DISC_REACH).astype(BF16),
    )


def query_row(block, projector, ones):
    channels = block.shape[1]
    probe = jnp.dot(block, projector[:, :channels], preferred_element_type=F32)
    return head_unit(probe.astype(BF16).astype(F32), ones).astype(BF16)


def lines_kernel(rows, reaches, profiles, source, payload, lines, staged, pad, sems):
    size = source.shape[0]
    fetch = pltpu.make_async_copy(source, staged.at[pl.ds(0, size), :], sems.at[0])
    fetch.start()
    shape = (FILTER_ROWS, pad.shape[1])
    lane = lax.broadcasted_iota(jnp.int32, shape, 1)
    for row in range(rows):
        pad[...] = jnp.zeros(shape, F32)
        pad[:BASIS_COUNT, : 3 * TAPS] = profiles[:, row, :]
        block = pad[...]
        straight = jnp.zeros(shape, F32)
        mirrored = jnp.zeros(shape, F32)
        for a in range(3):
            distance = jnp.abs(lane - (a * TAPS + CONV_REACH))
            seen = distance <= jnp.minimum(reaches[row, PATCH_LAT_EXTENT - 1 + a], CONV_REACH)
            part = jnp.where(seen, block, 0.0)
            shift = a * WINDOW + CONV_REACH - a * TAPS
            straight = straight + pltpu.roll(part, shift, 1)
            shift = (2 - a) * WINDOW + CONV_REACH - a * TAPS
            mirrored = mirrored + pltpu.roll(part, shift % pad.shape[1], 1)
        base = row * FILTER_ROWS
        straight = straight.astype(BF16)
        staged[size + base : size + base + FILTER_ROWS, :] = straight
        lines[0, base : base + FILTER_ROWS, :] = straight
        lines[1, base : base + FILTER_ROWS, :] = mirrored.astype(BF16)
    fetch.wait()
    send = pltpu.make_async_copy(staged, payload, sems.at[1])
    send.start()
    send.wait()


def fetches(pairs, sems):
    copies = [pltpu.make_async_copy(a, b, sems.at[i]) for i, (a, b) in enumerate(pairs)]
    for copy in copies:
        copy.start()
    return copies


def near_kernel(
    rows,
    longitudes,
    local,
    lines_hbm,
    partner,
    conv_gain_hbm,
    mixer_hbm,
    attn_gain_hbm,
    projector_hbm,
    hidden_out,
    keys_out,
    values_out,
    queries_out,
    lines,
    there,
    conv_gain,
    mixer,
    attn_gain,
    projector,
    raw,
    normed,
    filters,
    bands,
    basis,
    hidden,
    attn_in,
    keys,
    values,
    queries,
    sems,
    done,
):
    channels = raw.shape[2]
    size = rows * longitudes
    even = 1 - lax.rem(lax.axis_index("band"), 2)
    mine = (1 - even) * HALO
    other = HALO - mine
    near = 2 * HALO - 2
    own = (1 - even) * 2
    copies = fetches(
        [(local, raw.at[pl.ds(mine, HALO)])]
        + [
            (partner.at[pl.ds(row * longitudes, longitudes)], raw.at[other + row])
            for row in range(HALO)
        ]
        + [
            (conv_gain_hbm, conv_gain),
            (lines_hbm, lines),
            (partner.at[pl.ds(size, HALO * FILTER_ROWS)], there),
            (mixer_hbm, mixer),
            (attn_gain_hbm, attn_gain),
            (projector_hbm, projector),
        ],
        sems,
    )
    for copy in copies[:7]:
        copy.wait()
    for row in range(HALO):
        at = row * FILTER_ROWS
        filters[mine + row] = lines[0, at : at + FILTER_ROWS, :].astype(F32)
        filters[other + row] = there[at : at + FILTER_ROWS, :].astype(F32)
    norm_rows(2 * HALO, raw, normed, conv_gain)
    ones = head_ones(channels)
    for row in range(near):
        band_row(row, row + 1, normed, filters, bands.at[row % 2], basis.at[row])
    for copy in copies[7:]:
        copy.wait()
    for row in range(near):
        total = mix_row(raw[row + 1], basis.at[row], mixer)
        hidden[row] = total
        attn_in[row] = scaled_norm(total, attn_gain[...]).astype(BF16)
    sends = [pltpu.make_async_copy(hidden.at[pl.ds(own, 2)], hidden_out, done.at[0])]
    sends[0].start()
    for row in range(near):
        keys[row], values[row] = key_row(attn_in[row], projector, ones)
        sends += fetches(
            [(keys.at[row], keys_out.at[row]), (values.at[row], values_out.at[row])],
            done.at[pl.ds(1 + 2 * row, 2)],
        )
    for row in range(2):
        queries[row] = query_row(attn_in[own + row], projector, ones)
    sends += fetches([(queries, queries_out)], done.at[pl.ds(1 + 2 * near, 1)])
    for copy in sends:
        copy.wait()


def far_kernel(
    rows,
    longitudes,
    bands_count,
    reaches_hbm,
    scales_hbm,
    local,
    lines_hbm,
    cross,
    conv_gain_hbm,
    mixer_hbm,
    attn_gain_hbm,
    projector_hbm,
    final_hbm,
    near_hidden_hbm,
    near_keys,
    near_values,
    near_queries,
    out_hbm,
    reaches,
    scales,
    lines,
    there,
    conv_gain,
    mixer,
    attn_gain,
    projector,
    final,
    raw,
    normed,
    filters,
    bands,
    basis,
    hidden,
    attn_in,
    near_hidden,
    keys,
    values,
    queries,
    bias,
    mixture,
    out,
    sems,
    raw_sems,
    done,
):
    channels = raw.shape[2]
    size = rows * longitudes
    half = longitudes // 2
    position = lax.axis_index("band")
    pole = jnp.logical_or(position == 0, position == bands_count - 1)
    even = 1 - lax.rem(position, 2)
    wide = rows + 2 * PATCH_LAT_EXTENT
    near = 2 * HALO - 2
    far = wide - near
    far_base = (1 - even) * 2
    own_base = even * HALO
    far_slot = (1 - even) * near
    near_slot = even * far
    mine = even * 2
    mine_row = (1 - even) * 2
    copies = fetches(
        [
            (local.at[pl.ds(1 - even, 2)], raw.at[pl.ds(own_base, 2)]),
            (conv_gain_hbm, conv_gain),
            (lines_hbm, lines),
            (cross.at[pl.ds(size, HALO * FILTER_ROWS)], there),
        ],
        sems,
    )

    @pl.when(jnp.logical_not(pole))
    def received():
        fetched = fetches(
            [
                (cross.at[pl.ds(step * longitudes, longitudes)], raw.at[far_base + step])
                for step in range(HALO)
            ],
            raw_sems,
        )
        for copy in fetched:
            copy.wait()

    @pl.when(pole)
    def reflected():
        fetched = fetches(
            [
                (
                    local.at[HALO - 1 - step, pl.ds(side * half, half)],
                    raw.at[far_base + step, pl.ds((1 - side) * half, half)],
                )
                for step in range(HALO)
                for side in range(2)
            ],
            raw_sems,
        )
        for copy in fetched:
            copy.wait()

    copies += fetches(
        [
            (mixer_hbm, mixer),
            (attn_gain_hbm, attn_gain),
            (projector_hbm, projector),
            (near_queries, queries.at[pl.ds(even, 2)]),
            (near_keys, keys.at[pl.ds(near_slot, near)]),
            (near_values, values.at[pl.ds(near_slot, near)]),
            (near_hidden_hbm, near_hidden),
            (final_hbm, final),
            (reaches_hbm, reaches),
            (scales_hbm, scales),
        ],
        sems.at[pl.ds(4, 10)],
    )
    for copy in copies[:4]:
        copy.wait()

    def straight(row):
        return lines[0, row * FILTER_ROWS : (row + 1) * FILTER_ROWS, :].astype(F32)

    def outer(mirror, row):
        flipped = lines[1, mirror * FILTER_ROWS : (mirror + 1) * FILTER_ROWS, :].astype(F32)
        given = there[row * FILTER_ROWS : (row + 1) * FILTER_ROWS, :].astype(F32)
        return jnp.where(pole, flipped, given)

    for u in range(far):
        from_even = straight(0) if u == far - 1 else outer(far - 2 - u, u + 1)
        from_odd = straight(rows - 1) if u == 0 else outer(rows - u, u - 1)
        filters[u] = jnp.where(even > 0, from_even, from_odd)
    norm_rows(far + 2, raw, normed, conv_gain)
    ones = head_ones(channels)
    for row in range(far):
        band_row(row, row, normed, filters, bands.at[row % 2], basis.at[row])
    for copy in copies[4:]:
        copy.wait()
    for row in range(far):
        total = mix_row(raw[row + 1], basis.at[row], mixer)
        hidden[row] = total
        attn_in[row] = scaled_norm(total, attn_gain[...]).astype(BF16)
    for row in range(far):
        slot = far_slot + row
        keys[slot], values[slot] = key_row(attn_in[row], projector, ones)
    queries[mine_row] = query_row(attn_in[mine], projector, ones)
    lanes = HEAD_COUNT * QUERIES
    key_at = lax.broadcasted_iota(jnp.int32, (KEYS, lanes), 0)
    query_at = lax.broadcasted_iota(jnp.int32, (KEYS, lanes), 1) % QUERIES
    distance = jnp.abs(key_at - DISC_REACH - query_at)
    for row in range(rows):
        for a in range(DISC_ROWS):
            bias[row, a * KEYS : (a + 1) * KEYS, :] = jnp.where(
                distance <= reaches[row, a], 0.0, -1e30
            ).astype(F32)
    lane_head = lax.broadcasted_iota(jnp.int32, (1, lanes), 1) // QUERIES
    scale = jnp.zeros((1, lanes), F32)
    for h in range(HEAD_COUNT):
        scale = jnp.where(lane_head == h, scales[h], scale)
    channel_head = lax.broadcasted_iota(jnp.int32, (QUERIES, channels), 1) // HEAD_WIDTH

    def scores_of(row, start):
        probe = queries[row, pl.ds(start, QUERIES), :]
        spread = jnp.concatenate(
            [jnp.where(channel_head == h, probe, jnp.zeros_like(probe)) for h in range(HEAD_COUNT)],
            axis=0,
        )
        nearby = jnp.concatenate(
            [keys[row + a, pl.ds(start, KEYS), :] for a in range(DISC_ROWS)], axis=0
        )
        return lax.dot_general(
            nearby, spread, (((1,), (1,)), ((), ())), preferred_element_type=F32
        )

    def weights_of(row, scores):
        scores = scores + bias[row]
        peak = jnp.max(scores, axis=0, keepdims=True)
        weights = jnp.exp((scores - peak) * scale)
        total = jnp.sum(weights, axis=0, keepdims=True)
        return (weights * (1.0 / total)).astype(BF16)

    def mix(row, start, weights):
        nearby = jnp.concatenate(
            [values[row + a, pl.ds(start, KEYS), :] for a in range(DISC_ROWS)], axis=0
        )
        mixed = lax.dot_general(
            weights, nearby, (((0,), (0,)), ((), ())), preferred_element_type=F32
        )
        result = jnp.zeros((QUERIES, channels), F32)
        for h in range(HEAD_COUNT):
            result = jnp.where(channel_head == h, mixed[h * QUERIES : (h + 1) * QUERIES], result)
        mixture[row, pl.ds(start, QUERIES), :] = result.astype(BF16)

    per_row = longitudes // (QUERIES * UNROLL)

    def attend(step, carry):
        row = step // per_row
        base = (step % per_row) * (QUERIES * UNROLL)
        starts = [pl.multiple_of(base + u * QUERIES, QUERIES) for u in range(UNROLL)]
        scores = [scores_of(row, start) for start in starts]
        weights = [weights_of(row, block) for block in scores]
        for start, block in zip(starts, weights):
            mix(row, start, block)
        return carry

    lax.fori_loop(0, rows * per_row, attend, 0)
    sends = []
    for row in range(rows):
        product = jnp.dot(mixture[row], final[...], preferred_element_type=F32)
        slot = row - even
        far_own = hidden[mine]
        near_own = near_hidden[jnp.clip(slot, 0, 1)]
        own = jnp.where(row == mine_row, far_own, near_own)
        out[row] = (own + product).astype(BF16)
        sends += fetches([(out.at[row], out_hbm.at[row])], done.at[pl.ds(row, 1)])
    for copy in sends:
        copy.wait()


def on_device(
    grid_inputs,
    stencil_prenorm_scale,
    patch_kernel_profiles,
    channel_mixer_tensor,
    softmax_prenorm_scale,
    probe_lookup_content_projector,
    head_logit_scales,
    final_projector,
    azimuth_reaches,
):
    rows, longitudes, channels = grid_inputs.shape
    count = lax.axis_size("band")
    assert rows == HALO and longitudes % (QUERIES * UNROLL) == 0
    assert longitudes % BAND == 0 and channels == 256 and count % 2 == 0
    within = [(i, i ^ 1) for i in range(count)]
    across = [pair for i in range(1, count - 1, 2) for pair in ((i, i + 1), (i + 1, i))]
    size = rows * longitudes
    flat = grid_inputs.reshape(size, channels)
    smem = pl.BlockSpec(memory_space=pltpu.SMEM)
    vmem = pl.BlockSpec(memory_space=pltpu.VMEM)
    hbm = pl.BlockSpec(memory_space=pltpu.HBM)
    limit = pltpu.CompilerParams(vmem_limit_bytes=VMEM_LIMIT)
    lines_shape = (2, rows * FILTER_ROWS, channels)
    payload, lines = pl.pallas_call(
        functools.partial(lines_kernel, rows),
        out_shape=(
            jax.ShapeDtypeStruct((size + rows * FILTER_ROWS, channels), BF16),
            jax.ShapeDtypeStruct(lines_shape, BF16),
        ),
        in_specs=[smem, vmem, hbm],
        out_specs=(hbm, vmem),
        scratch_shapes=[
            pltpu.VMEM((size + rows * FILTER_ROWS, channels), BF16),
            pltpu.VMEM((FILTER_ROWS, channels), F32),
            pltpu.SemaphoreType.DMA((2,)),
        ],
    )(azimuth_reaches, patch_kernel_profiles.transpose(1, 0, 2), flat)
    cross = lax.ppermute(payload, "band", across)
    partner = lax.ppermute(payload, "band", within)
    conv_gain = stencil_prenorm_scale.reshape(1, channels)
    attn_gain = softmax_prenorm_scale.reshape(1, channels)
    near = 2 * HALO - 2
    wide = rows + 2 * PATCH_LAT_EXTENT
    far = wide - near
    padded = longitudes + 2 * DISC_REACH
    sources = [
        pltpu.VMEM(lines_shape, BF16),
        pltpu.VMEM((HALO * FILTER_ROWS, channels), BF16),
        pltpu.VMEM((1, channels), F32),
        pltpu.VMEM(channel_mixer_tensor.shape, BF16),
        pltpu.VMEM((1, channels), F32),
        pltpu.VMEM(probe_lookup_content_projector.shape, BF16),
    ]

    def working(count):
        return [
            pltpu.VMEM((count + 2, longitudes, channels), BF16),
            pltpu.VMEM((count + 2, longitudes + 32, channels), BF16),
            pltpu.VMEM((count + 2, FILTER_ROWS, channels), F32),
            pltpu.VMEM((2, BASIS_COUNT * BAND, channels), BF16),
            pltpu.VMEM((count, longitudes, BASIS_COUNT * channels), BF16),
            pltpu.VMEM((count, longitudes, channels), F32),
            pltpu.VMEM((count, longitudes, channels), BF16),
        ]

    near_state = pl.pallas_call(
        functools.partial(near_kernel, rows, longitudes),
        out_shape=(
            jax.ShapeDtypeStruct((2, longitudes, channels), F32),
            jax.ShapeDtypeStruct((near, padded, channels), BF16),
            jax.ShapeDtypeStruct((near, padded, channels), BF16),
            jax.ShapeDtypeStruct((2, longitudes, channels), BF16),
        ),
        in_specs=[hbm] * 7,
        out_specs=(hbm,) * 4,
        scratch_shapes=sources
        + working(near)
        + [
            pltpu.VMEM((near, padded, channels), BF16),
            pltpu.VMEM((near, padded, channels), BF16),
            pltpu.VMEM((2, longitudes, channels), BF16),
            pltpu.SemaphoreType.DMA((10,)),
            pltpu.SemaphoreType.DMA((2 + 2 * near,)),
        ],
        compiler_params=limit,
        cost_estimate=pl.CostEstimate(flops=8 * 10**9, bytes_accessed=8 * 10**6, transcendentals=0),
    )(
        grid_inputs,
        lines,
        partner,
        conv_gain,
        channel_mixer_tensor,
        attn_gain,
        probe_lookup_content_projector,
    )
    return pl.pallas_call(
        functools.partial(far_kernel, rows, longitudes, count),
        out_shape=jax.ShapeDtypeStruct(grid_inputs.shape, BF16),
        in_specs=[hbm] * 14,
        out_specs=hbm,
        scratch_shapes=[
            pltpu.SMEM(azimuth_reaches.shape, jnp.int32),
            pltpu.SMEM(head_logit_scales.shape, F32),
        ]
        + sources
        + [pltpu.VMEM(final_projector.shape, BF16)]
        + working(far)
        + [
            pltpu.VMEM((2, longitudes, channels), F32),
            pltpu.VMEM((wide, padded, channels), BF16),
            pltpu.VMEM((wide, padded, channels), BF16),
            pltpu.VMEM((rows, longitudes, channels), BF16),
            pltpu.VMEM((rows, DISC_ROWS * KEYS, HEAD_COUNT * QUERIES), F32),
            pltpu.VMEM((rows, longitudes, channels), BF16),
            pltpu.VMEM((rows, longitudes, channels), BF16),
            pltpu.SemaphoreType.DMA((14,)),
            pltpu.SemaphoreType.DMA((2 * HALO,)),
            pltpu.SemaphoreType.DMA((rows,)),
        ],
        compiler_params=limit,
        cost_estimate=pl.CostEstimate(flops=10**10, bytes_accessed=8 * 10**6, transcendentals=10**6),
    )(
        azimuth_reaches,
        head_logit_scales,
        grid_inputs,
        lines,
        cross,
        conv_gain,
        channel_mixer_tensor,
        attn_gain,
        probe_lookup_content_projector,
        final_projector,
        *near_state,
    )


def solution(mesh):
    placed = (
        P(("members", "band"), None, None),
        P(),
        P("band", None, None),
        P(),
        P(),
        P(),
        P(),
        P(),
        P("band", None),
    )
    return jax.shard_map(
        on_device,
        mesh=mesh,
        in_specs=placed,
        out_specs=P(("members", "band"), None, None),
        check_vma=False,
    )
```

time: 55.2 us -> 35.2 us (0.64)
  the two profiles are of different devices: /device:TPU:5 before, /device:TPU:25 now
where the time goes in v3:
time: 35.2 us; the launch traced here: 34.9 us
  Pallas kernels  24.5 us (70%)
  waiting for transfers between devices  6.64 us (19%)
  starting transfers between devices  3.79 us (11%)
    pallas_call x1, Pallas kernels, on_device(): pl.pallas_call(functools.partial(far_kernel, rows, longitudes, count), ou...  12.6 us
    pallas_call x1, Pallas kernels, on_device(): pl.pallas_call(functools.partial(near_kernel, rows, longitudes), out_shap...  8.64 us
    ppermute x1, waiting for transfers between devices, on_device(): cross = lax.ppermute(payload, 'band', across)  6.64 us
    pallas_call x1, Pallas kernels, on_device(): pl.pallas_call(functools.partial(lines_kernel, rows), out_shape=(jax.Shap...  3.27 us
    ppermute x1, starting transfers between devices, on_device(): cross = lax.ppermute(payload, 'band', across)  3.05 us
    ppermute x1, starting transfers between devices, on_device(): partner = lax.ppermute(payload, 'band', within)  0.74 us
  transfers between devices with their start and end apart: 2, of which 1 were waited for; matrix products, arithmetic and copies ran while one was open for 0% of the time, Pallas kernels for 25%

profile of v3, /device:TPU:25, one launch (start us, length us, event | category | flops | bytes accessed | tf_op | source)
XLA Modules:
  0.0 34.9 jit_solution(9473276158749502)
XLA Ops:
  0.0 3.3 %shard_map.91 = (bf16[1200,256]{1,0:T(8,128)(2,1)}, bf16[2,48,256]{2,1,0:T(8,128)(2,1)}) custom-call(s32[3,5]{1,0:T(4,128)} %reaches_hbm.1, f32[9,3,27]{2,1,0:T(4,128)} %bitcast.5, bf16[1152,256]{1,0:T(8,128)(2,1)} %bitcast.4), custom_call_target="tpu_custom_call" | custom-call | tf_op jit(solution)/shard_map/pallas_call | solution.py:480
  3.3 0.7 %collective-permute-start.1 = (bf16[1200,256]{1,0:T(8,128)(2,1)}, bf16[1200,256]{1,0:T(8,128)(2,1)}, u32[]{:S(2)}, u32[]{:S(2)}) collective-permute-start(bf16[1200,256]{1,0:T(8,128)(2,1)} %get-tuple-element.12), channel_id=1, source_target_pairs={{0,1},{1,0},{2,3},{3,2},{4,5},{5,4},{6,7},{7,6},{8,9},{9,8},{10,11... | collective-permute-start | bytes 1843208 | tf_op jit(solution)/shard_map/ppermute | solution.py:495
  4.0 3.0 %collective-permute-start = (bf16[1200,256]{1,0:T(8,128)(2,1)}, bf16[1200,256]{1,0:T(8,128)(2,1)}, u32[]{:S(2)}, u32[]{:S(2)}) collective-permute-start(bf16[1200,256]{1,0:T(8,128)(2,1)} %get-tuple-element.12), channel_id=1, source_target_pairs={{1,2},{2,1},{3,4},{4,3},{5,6},{6,5},{7,8},{8,7},{9,10},{10,9},{11,... | collective-permute-start | bytes 1843208 | tf_op jit(solution)/shard_map/ppermute | solution.py:494
  7.1 0.0 collective-permute-done.1.partner
  7.1 8.6 %shard_map.92 = (f32[2,384,256]{2,1,0:T(8,128)}, bf16[4,400,256]{2,1,0:T(8,128)(2,1)}, bf16[4,400,256]{2,1,0:T(8,128)(2,1)}, bf16[2,384,256]{2,1,0:T(8,128)(2,1)}) custom-call(bf16[3,384,256]{2,1,0:T(8,128)(2,1)} %local.3, bf16[2,48,256]{2,1,0:T(8,128)(2,1)} %get-tuple-element.11.lines_hbm, bf16[1200,256]{1,0:T(8,128)(2,1)} %collective-permute-done.1.partner, ...), custom_call_target="tpu_custom_call" | custom-call | flops 8000000000 | bytes 8000000 | tf_op jit(solution)/shard_map/pallas_call | solution.py:522
  15.7 6.6 %collective-permute-done.cross = bf16[1200,256]{1,0:T(8,128)(2,1)} collective-permute-done((bf16[1200,256]{1,0:T(8,128)(2,1)}, bf16[1200,256]{1,0:T(8,128)(2,1)}, u32[]{:S(2)}, u32[]{:S(2)}) %collective-permute-start) | collective-permute-done | bytes 614432 | tf_op jit(solution)/shard_map/ppermute | solution.py:494
  22.4 12.6 %shard_map.93 = bf16[3,384,256]{2,1,0:T(8,128)(2,1)} custom-call(s32[3,5]{1,0:T(4,128)} %reaches_hbm.1, f32[8]{0:T(128)} %scales_hbm.1, bf16[3,384,256]{2,1,0:T(8,128)(2,1)} %local.3, bf16[2,48,256]{2,1,0:T(8,128)(2,1)} %get-tuple-element.11.lines_hbm, bf16[1200,256]{1,0:T(8,128)(2,1)} %collective-permute-done.cross, f32[1,256]{1,0:T(1,128)} %bitcast.7, ...), custom_call_target="tpu_custom_call" | custom-call | flops 10000000000 | bytes 8000000 | tf_op jit(solution)/shard_map/pallas_call | solution.py:552
Async XLA Ops:
  3.3 3.8 %collective-permute-start.1 = (bf16[1200,256]{1,0:T(8,128)(2,1)}, bf16[1200,256]{1,0:T(8,128)(2,1)}, u32[]{:S(2)}, u32[]{:S(2)}) collective-permute-start(bf16[1200,256]{1,0:T(8,128)(2,1)} %get-tuple-element.12), channel_id=1, source_target_pairs={{0,1},{1,0},{2,3},{3,2},{4,5},{5,4},{6,7},{7,6},{8,9},{9,8},{10,11... | collective-permute-start | bytes 1843208 | tf_op jit(solution)/shard_map/ppermute | solution.py:495
  4.0 18.4 %collective-permute-start = (bf16[1200,256]{1,0:T(8,128)(2,1)}, bf16[1200,256]{1,0:T(8,128)(2,1)}, u32[]{:S(2)}, u32[]{:S(2)}) collective-permute-start(bf16[1200,256]{1,0:T(8,128)(2,1)} %get-tuple-element.12), channel_id=1, source_target_pairs={{1,2},{2,1},{3,4},{4,3},{5,6},{6,5},{7,8},{8,7},{9,10},{10,9},{11,... | collective-permute-start | bytes 1843208 | tf_op jit(solution)/shard_map/ppermute | solution.py:494
